TPU v7x, 32 devices: a whole 2x2x4 slice. The times are simulated.
32 devices in a mesh: rows: 8 (over z, core), seq: 4 (over y, x).
Axes of the slice: x: 2, y: 2, z: 4, core: 2. Of those that a mesh axis runs over, the one named last changes fastest.
Arguments:
- byte_ids: int32 [64, 2048], P('rows', 'seq'), may hold values from 0 to 255
- segment_ids: int32 [64, 2048], P('rows', 'seq'), may hold values from 0 to 7, never falling along the last dimension, each value on 1 to 1024 neighbouring positions
- table: bfloat16 [256, 768], replicated, may hold values from -6 to 6
- conv_weight: bfloat16 [4, 768], replicated, may hold values from -3 to 3
- scorer: bfloat16 [768], replicated, may hold values from -0.4375 to 0.4375
- cotangent: bfloat16 [64, 1024, 768], P('rows', 'seq'), may hold values from -6 to 6
Outputs:
- blocks_out: bfloat16 [64, 1024, 768], P('rows', 'seq')
- table_grad: float32 [256, 768], P('seq')
- conv_grad: float32 [4, 768], replicated
- scorer_grad: float32 [768], replicated
Inputs may be any that keep to these rules, and one draw needn't show every extreme that they name: `segment_ids`: within each row the numbers never fall; a document spans at most 1024 bytes and may cross from one piece of the row to the next.
All inputs are finite; a program needn't handle non-finite values.
Results may differ from a plain program's by a relative error of at most 0.001.
Values sent between devices are 32-bit elements; how exact they have to be, the bound alone decides.
No kernel may reach another device: no remote copies, remote signals or barrier semaphores. Data moves between devices by JAX's collectives and lax.ppermute only.
A program may use at most 320 MiB of HBM per device.

v0:
```python
import jax
import jax.numpy as jnp
from jax import lax
from jax.sharding import PartitionSpec as P


def passed_along(shard, axis, by):
    length = lax.axis_size(axis)
    pairs = [(i, i + by) for i in range(length) if 0 <= i + by < length]
    return lax.ppermute(shard, axis, pairs)


def pad_positions(value, before, after):
    return jnp.pad(value, ((0, 0), (before, after), (0, 0)))


def per_device(byte_ids, segment_ids, table, conv_weight, scorer, cotangent):
    rows_here, group = byte_ids.shape
    vocab, width = table.shape
    kernel = conv_weight.shape[0]
    reach = kernel - 1
    pool_reach = 3
    margin = reach + pool_reach
    tails = passed_along(
        (byte_ids[:, group - margin :], segment_ids[:, group - margin :]), "seq", 1
    )
    seg_rim = jnp.where(lax.axis_index("seq") == 0, -1, tails[1])
    bytes_ext = jnp.concatenate([tails[0], byte_ids], axis=1)
    seg_ext = jnp.concatenate([seg_rim, segment_ids], axis=1)
    onehot_ext = (bytes_ext[:, :, None] == jnp.arange(vocab, dtype=jnp.int32)).astype(jnp.bfloat16)
    embedded = jnp.einsum("rcv,vd->rcd", onehot_ext, table, preferred_element_type=jnp.float32)
    weights32 = conv_weight.astype(jnp.float32)
    scorer32 = scorer.astype(jnp.float32)
    span = group + pool_reach
    conv_masks = []
    conved = jnp.zeros((rows_here, span, width), jnp.float32)
    for offset in range(kernel):
        same_doc = (
            seg_ext[:, reach - offset : reach - offset + span] == seg_ext[:, reach : reach + span]
        ).astype(jnp.float32)
        conv_masks.append(same_doc)
        conved = (
            conved
            + weights32[offset]
            * embedded[:, reach - offset : reach - offset + span]
            * same_doc[:, :, None]
        )
    pool_masks = []
    pooled = []
    counts = []
    running = jnp.zeros((rows_here, group, width), jnp.float32)
    counted = jnp.zeros((rows_here, group), jnp.float32)
    for offset in range(pool_reach + 1):
        same_doc = (
            seg_ext[:, margin - offset : margin - offset + group]
            == seg_ext[:, margin : margin + group]
        ).astype(jnp.float32)
        pool_masks.append(same_doc)
        running = (
            running
            + same_doc[:, :, None] * conved[:, pool_reach - offset : pool_reach - offset + group]
        )
        counted = counted + same_doc
        counts.append(counted)
        pooled.append(running / counted[:, :, None])
    scores = jnp.stack(
        [
            jnp.einsum("rcd,d->rc", level, scorer32, precision=lax.Precision.HIGHEST)
            for level in pooled
        ]
    )
    probs = jax.nn.softmax(scores, axis=0)
    mixed = sum((probs[level][:, :, None] * pooled[level] for level in range(len(pooled))))
    blocks_out = jnp.mean(mixed.reshape(rows_here, group // 2, 2, width), axis=2).astype(
        jnp.bfloat16
    )
    grad_mixed = jnp.repeat(0.5 * cotangent.astype(jnp.float32), 2, axis=1)
    grad_prob = jnp.stack([jnp.sum(grad_mixed * level, axis=-1) for level in pooled])
    average = jnp.sum(probs * grad_prob, axis=0)
    grad_score = probs * (grad_prob - average)
    grad_scorer = sum(
        (
            jnp.einsum(
                "rc,rcd->d", grad_score[level], pooled[level], precision=lax.Precision.HIGHEST
            )
            for level in range(len(pooled))
        )
    )
    grad_conved = jnp.zeros((rows_here, span, width), jnp.float32)
    carried = jnp.zeros((rows_here, group, width), jnp.float32)
    for offset in range(pool_reach, -1, -1):
        grad_pooled = (
            probs[offset][:, :, None] * grad_mixed + grad_score[offset][:, :, None] * scorer32
        )
        carried = carried + grad_pooled / counts[offset][:, :, None]
        grad_conved = grad_conved + pad_positions(
            pool_masks[offset][:, :, None] * carried, pool_reach - offset, offset
        )
    grad_weight_rows = []
    grad_embedded = jnp.zeros((rows_here, group + margin, width), jnp.float32)
    for offset in range(kernel):
        masked_grad = grad_conved * conv_masks[offset][:, :, None]
        grad_weight_rows.append(
            jnp.sum(masked_grad * embedded[:, reach - offset : reach - offset + span], axis=(0, 1))
        )
        grad_embedded = grad_embedded + pad_positions(
            weights32[offset] * masked_grad, reach - offset, offset
        )
    grad_weight = jnp.stack(grad_weight_rows)
    returned = passed_along(grad_embedded[:, :margin], "seq", -1)
    own_grad = grad_embedded[:, margin:]
    own_grad = jnp.concatenate(
        [own_grad[:, : group - margin], own_grad[:, group - margin :] + returned], axis=1
    )
    grad_table = jnp.einsum(
        "rcv,rcd->vd",
        onehot_ext[:, margin:].astype(jnp.float32),
        own_grad,
        precision=lax.Precision.HIGHEST,
    )
    share = vocab // lax.axis_size("seq")
    totals = lax.psum((grad_table, grad_weight, grad_scorer), ("rows", "seq"))
    table_grad = lax.dynamic_slice_in_dim(totals[0], lax.axis_index("seq") * share, share, 0)
    conv_grad = totals[1]
    scorer_grad = totals[2]
    return (blocks_out, table_grad, conv_grad, scorer_grad)


def solution(mesh):
    return jax.shard_map(
        per_device,
        mesh=mesh,
        in_specs=(P("rows", "seq"), P("rows", "seq"), P(), P(), P(), P("rows", "seq", None)),
        out_specs=(P("rows", "seq", None), P("seq", None), P(), P()),
        check_vma=False,
    )
```

profile of v0, /device:TPU:0, one launch (start us, length us, event | category | flops | bytes accessed | tf_op | source)
XLA Modules:
  0.0 531.4 jit_solution(9029548623649306104)
XLA Ops:
  7.2 0.0 copy-start
  7.2 0.0 all-reduce.11.cloned.1.call-start
  7.2 0.8 slice.127
  8.0 4.9 collective-permute-start.1
  12.9 0.8 slice.123
  13.7 3.4 collective-permute-start
  17.1 0.7 reshape.58
  17.7 0.7 convert_element_type.60
  18.4 0.7 convert_element_type.51
  19.2 2.5 convert_multiply_fusion
  21.6 6.5 %broadcast_in_dim.7 = f32[8,256,2,768]{3,2,1,0:T(2,128)} broadcast(f32[8,256,768]{2,1,0:T(8,128)S(1)} %convert_multiply_fusion), dimensions={0,1,3} | broadcast | bytes 18874368 | tf_op jit(solution)/shard_map/broadcast_in_dim | solution.py:77
  28.1 15.8 %reshape.56 = f32[8,512,768]{2,1,0:T(8,128)} reshape(f32[8,256,2,768]{3,2,1,0:T(2,128)} %broadcast_in_dim.7) | data formatting | bytes 25165824 | tf_op jit(solution)/shard_map/reshape | solution.py:77
  43.9 0.1 broadcast_add_fusion
  44.0 0.1 fusion.54
  44.1 0.1 fusion.35
  44.2 0.1 pad_add_fusion.3
  44.3 1.8 iota_compare_fusion
  46.1 2.6 fusion.22
  48.7 10.7 %multiply_add_fusion = f32[8,515,768]{2,1,0:T(8,128)} fusion(f32[8,518,768]{2,1,0:T(8,128)S(1)} %fusion.22, f32[8,515]{1,0:T(8,128)S(1)} %get-tuple-element.52, f32[768]{0:T(1024)S(1)} %get-tuple-element.13, f32[8,515]{1,0:T(8,128)S(1)} %get-tuple-element.51, f32[768]{0:T(1024)S(1)} %get-tuple-element.14, f32[8,515]{1,0:T(8,128)S(1)} %get-tuple-element.50, ...), kind=kLoop, calls=%fused_computation.6 | loop fusion | flops 31641600 | bytes 63344928 | tf_op jit(solution)/shard_map/add | solution.py:43
  59.4 9.0 %fusion.10 = f32[1,8,512]{2,0,1:T(1,128)S(1)} fusion(bf16[768,1,1]{0,1,2:T(2,128)(2,1)S(1)} %reshape.58, f32[8,515,768]{2,1,0:T(8,128)} %multiply_add_fusion), kind=kOutput, calls=%fused_computation.32 | convolution fusion | flops 37748736 | bytes 12600832 | tf_op jit(solution)/shard_map/rcd,d->rc/dot_general | solution.py:68
  68.5 35.6 %multiply_reduce_fusion.7 = (f32[8,512]{1,0:T(8,128)S(1)}, f32[8,512]{1,0:T(8,128)S(1)}, f32[8,512]{1,0:T(8,128)S(1)}, f32[8,512]{1,0:T(8,128)S(1)}, f32[8,512,7...) fusion(f32[8,512,768]{2,1,0:T(8,128)} %reshape.56, f32[8,515,768]{2,1,0:T(8,128)} %multiply_add_fusion, ...), kind=kLoop, calls=%fused_computation.25 | loop fusion | flops 53460992 | bytes 100827136 | tf_op jit(solution)/shard_map/reduce_sum | solution.py:78
  104.1 10.3 %fusion.58 = f32[1,8,512]{2,0,1:T(1,128)S(1)} fusion(f32[8,512,768]{2,1,0:T(8,128)} %get-tuple-element.21, bf16[768,1,1]{0,1,2:T(2,128)(2,1)S(1)} %reshape.58), kind=kOutput, calls=%fused_computation.124 | convolution fusion | flops 37748736 | bytes 12600832 | tf_op jit(solution)/shard_map/rcd,d->rc/dot_general | solution.py:68
  114.4 5.9 %fusion.59 = f32[1,8,512]{2,0,1:T(1,128)S(1)} fusion(f32[8,512,768]{2,1,0:T(8,128)S(1)} %copy-done.4, bf16[768,1,1]{0,1,2:T(2,128)(2,1)S(1)} %reshape.58), kind=kOutput, calls=%fused_computation.125 | convolution fusion | flops 37748736 | bytes 12600832 | tf_op jit(solution)/shard_map/rcd,d->rc/dot_general | solution.py:68
  120.3 0.0 slice-start.3
  120.3 10.9 %fusion.50 = f32[1,8,512]{2,0,1:T(1,128)S(1)} fusion(bf16[768,1,1]{0,1,2:T(2,128)(2,1)S(1)} %reshape.58, f32[8,512,768]{2,1,0:T(8,128)} %get-tuple-element.23, f32[8,512]{1,0:T(8,128)S(1)} %get-tuple-element.24), kind=kOutput, calls=%fused_computation.122 | convolution fusion | flops 40894464 | bytes 12617216 | tf_op jit(solution)/shard_map/rcd,d->rc/dot_general | solution.py:68
  131.4 18.1 %multiply_add_fusion.1 = f32[8,512,768]{2,1,0:T(8,128)} fusion(f32[8,512,768]{2,1,0:T(8,128)} %get-tuple-element.22, f32[8,512,768]{2,1,0:T(8,128)} %get-tuple-element.21, f32[8,515,768]{2,1,0:T(8,128)S(1)} %bitcast.54, f32[8,512]{1,0:T(8,128)S(1)} %get-tuple-element.47, f32[8,512]{1,0:T(8,128)S(1)} %get-tuple-element.48, ...), kind=kLoop, calls=%fused_computation.26 | loop fusion | flops 25165824 | bytes 62996480 | tf_op jit(solution)/shard_map/add | solution.py:73
  149.5 20.0 %broadcast_multiply_fusion.2 = (f32[8,512,768]{2,1,0:T(8,128)}, f32[8,512,768]{2,1,0:T(8,128)}, f32[8,512,768]{2,1,0:T(8,128)}, f32[8,512,768]{2,1,0:T(8,128)}) fusion(f32[8,512]{1,0:T(8,128)S(1)} %get-tuple-element.25, f32[8,512]{1,0:T(8,128)S(1)} %get-tuple-element.24, f32[768]{0:T(1024)S(1)} %convert_element_type.60, f32[8,512]{1,0:T(8,128)S(1)} %get-tuple-element.43, ...), kind=kLoop, calls=%fused_computation.41 | loop fusion | flops 66060288 | bytes 63147008 | tf_op jit(solution)/shard_map/mul | solution.py:97
  169.5 41.9 %multiply_reduce_fusion.3 = (f32[768]{0:T(1024)S(1)}, f32[768]{0:T(1024)S(1)}, f32[768]{0:T(1024)S(1)}, f32[768]{0:T(1024)S(1)}, f32[8,515,768]{2,1,0:T(8,128)}) fusion(f32[8,518,768]{2,1,0:T(8,128)} %copy-done.2, f32[8,515]{1,0:T(8,128)S(1)} %get-tuple-element.50, f32[8,515]{1,0:T(8,128)S(1)} %get-tuple-element.51, f32[8,515]{1,0:T(8,128)S(1)} %get-tuple-element.52, ...), kind=kLoop, calls=%fused_computation.3 | loop fusion | flops 44295168 | bytes 113676576 | tf_op jit(solution)/shard_map/reduce_sum | solution.py:104
  211.4 16.9 %broadcast_multiply_fusion = (f32[8,515,768]{2,1,0:T(8,128)S(1)}, f32[8,515,768]{2,1,0:T(8,128)}, f32[8,515,768]{2,1,0:T(8,128)}, f32[8,515,768]{2,1,0:T(8,128)}) fusion(f32[8,515,768]{2,1,0:T(8,128)} %get-tuple-element.18, f32[768]{0:T(1024)S(1)} %get-tuple-element.12, f32[8,515]{1,0:T(8,128)S(1)} %get-tuple-element.52, f32[768]{0:T(1024)S(1)} %get-tuple-element.13, ...), kind=kLoop, calls=%fused_computation.35 | loop fusion | flops 22149120 | bytes 63344928 | tf_op jit(solution)/shard_map/mul | solution.py:107
  228.3 4.6 copy-done.3
  232.9 1.2 pad_add_fusion.2
  234.1 22.6 %pad_add_fusion = f32[8,518,768]{2,1,0:T(8,128)} fusion(f32[8,515,768]{2,1,0:T(8,128)} %get-tuple-element.31, f32[8,515,768]{2,1,0:T(8,128)} %get-tuple-element.32, f32[8,515,768]{2,1,0:T(8,128)} %get-tuple-element.33, f32[8,515,768]{2,1,0:T(8,128)} %copy-done.3), kind=kLoop, calls=%fused_computation.4 | loop fusion | flops 9547776 | bytes 63356928 | tf_op jit(solution)/shard_map/add | solution.py:106
  256.7 9.9 %convolution_reduce_fusion.2 = f32[768]{0:T(1024)S(1)} fusion(f32[8,512,1]{1,0,2:T(8,128)S(1)} %get-tuple-element.38, f32[8,512,768]{2,1,0:T(8,128)} %get-tuple-element.23, f32[8,512]{1,0:T(8,128)S(1)} %get-tuple-element.24), kind=kOutput, calls=%fused_computation.47 | convolution fusion | flops 40894464 | bytes 12618752 | tf_op jit(solution)/shard_map/rc,rcd->d/dot_general | solution.py:83
  266.6 6.7 %fusion.19 = f32[768]{0:T(1024)S(1)} fusion(f32[8,515,768]{2,1,0:T(8,128)S(1)} %bitcast.56, f32[8,512,1]{1,0,2:T(8,128)S(1)} %get-tuple-element.41), kind=kOutput, calls=%fused_computation.48 | convolution fusion | flops 37748736 | bytes 12602368 | tf_op jit(solution)/shard_map/rc,rcd->d/dot_general | solution.py:83
  273.4 9.4 %convolution_reduce_fusion.1 = f32[768]{0:T(1024)S(1)} fusion(f32[8,512,768]{2,1,0:T(8,128)} %get-tuple-element.21, f32[8,512,1]{1,0,2:T(8,128)S(1)} %get-tuple-element.40), kind=kOutput, calls=%fused_computation.46 | convolution fusion | flops 37748736 | bytes 12602368 | tf_op jit(solution)/shard_map/rc,rcd->d/dot_general | solution.py:83
  282.9 6.0 %convolution_reduce_fusion = f32[768]{0:T(1024)S(1)} fusion(f32[8,512,768]{2,1,0:T(8,128)S(1)} %bitcast.58, f32[8,512,1]{1,0,2:T(8,128)S(1)} %get-tuple-element.39), kind=kOutput, calls=%fused_computation.45 | convolution fusion | flops 37748736 | bytes 12602368 | tf_op jit(solution)/shard_map/rc,rcd->d/dot_general | solution.py:83
  288.8 1.3 collective-permute-start.2
  290.2 15.1 %reshape.55 = f32[8,256,2,768]{3,2,1,0:T(2,128)} reshape(f32[8,512,768]{2,1,0:T(8,128)} %multiply_add_fusion.1) | data formatting | bytes 25165824 | tf_op jit(solution)/shard_map/reshape | solution.py:74
  305.3 10.5 %slice.188 = f32[8,506,768]{2,1,0:T(8,128)} slice(f32[8,518,768]{2,1,0:T(8,128)} %pad_add_fusion), slice={[0:8], [6:512], [0:768]} | slice | bytes 24870912 | tf_op jit(solution)/shard_map/slice | solution.py:113
  315.8 19.5 %reduce_sum.100 = f32[8,256,768]{2,1,0:T(8,128)} reduce(f32[8,256,2,768]{3,2,1,0:T(2,128)} %reshape.55, f32[]{:T(128)} %constant.12.clone.1), dimensions={2}, to_apply=%region_1.2 | reduce | flops 1572864 | bytes 18874372 | tf_op jit(solution)/shard_map/reduce_sum | solution.py:74
  335.3 41.5 %all-reduce.8 = (f32[4,768]{1,0:T(4,128)}, f32[768]{0:T(1024)}) all-reduce(f32[4,768]{1,0:T(4,128)S(1)} %pad_maximum_fusion.1, f32[768]{0:T(1024)S(1)} %add_add_fusion.2), channel_id=1, replica_groups=mesh['rows'=8,'seq'=4] {'rows','seq'}, use_global_device_ids=true, to_apply=%region_12.13 | all-reduce | flops 3840 | bytes 30720 | tf_op jit(solution)/shard_map/psum | solution.py:122
  376.8 1.5 add_add_fusion.1
  378.4 0.2 copy-done.5
  378.6 12.4 %fusion.14 = f32[256,768]{1,0:T(8,128)} fusion(f32[8,6,768]{2,1,0:T(8,128)S(1)} %add_add_fusion.1, f32[8,506,768]{2,1,0:T(8,128)} %slice.188, pred[8,518,256]{1,2,0:T(32,128)(4,1)S(1)} %copy-done.5), kind=kOutput, calls=%fused_computation.44 | convolution fusion | flops 9666822144 | bytes 14467072 | tf_op jit(solution)/shard_map/rcv,rcd->vd/dot_general | solution.py:115
  391.0 0.0 all-reduce.11.cloned.1.call-update
  391.0 5.0 multiply_convert_fusion
  396.0 126.7 %all-reduce.11.cloned.1.call-done = f32[256,768]{1,0:T(8,128)} async-done(((f32[256,768]{1,0:T(8,128)}), f32[256,768]{1,0:T(8,128)}) %all-reduce.11.cloned.1.call-update) | async-done | bytes 786448 | tf_op jit(solution)/shard_map/psum | solution.py:122
  522.7 1.6 constant_dynamic-slice_fusion
  (58 shorter events, 0.3 us)
Async XLA Ops:
  7.2 38.9 %copy-start = (bf16[256,768]{1,0:T(8,128)(2,1)S(1)}, bf16[256,768]{1,0:T(8,128)(2,1)}, u32[]{:S(2)}) copy-start(bf16[256,768]{1,0:T(8,128)(2,1)} %param.8) | copy-start | bytes 1179652
  7.2 515.6 %all-reduce.11.cloned.1.call-start = ((), (), s32[]{:S(2)}) async-start(), calls=%async_computation | async-start | bytes 1572864 | tf_op jit(solution)/shard_map/psum | solution.py:122
  8.0 35.9 %collective-permute-start.1 = (s32[8,6]{1,0:T(8,128)S(1)}, s32[8,6]{1,0:T(8,128)S(1)}, u32[]{:S(2)}, u32[]{:S(2)}) collective-permute-start(s32[8,6]{1,0:T(8,128)S(1)} %slice.127), channel_id=1, source_target_pairs={{0,1},{1,2},{2,3},{4,5},{5,6},{6,7},{8,9},{9,10},{10,11},{12,13},{... | collective-permute-start | bytes 584 | tf_op jit(solution)/shard_map/ppermute | solution.py:10
  13.7 30.6 %collective-permute-start = (s32[8,6]{1,0:T(8,128)S(1)}, s32[8,6]{1,0:T(8,128)S(1)}, u32[]{:S(2)}, u32[]{:S(2)}) collective-permute-start(s32[8,6]{1,0:T(8,128)S(1)} %slice.123), channel_id=1, source_target_pairs={{0,1},{1,2},{2,3},{4,5},{5,6},{6,7},{8,9},{9,10},{10,11},{12,13},{... | collective-permute-start | bytes 584 | tf_op jit(solution)/shard_map/ppermute | solution.py:10
  28.1 15.8 %copy-start.6 = (s32[8,512]{1,0:T(8,128)S(1)}, s32[8,512]{1,0:T(8,128)}, u32[]{:S(2)}) copy-start(s32[8,512]{1,0:T(8,128)} %param.7) | copy-start | bytes 49156
  28.1 16.1 %copy-start.7 = (s32[8,512]{1,0:T(8,128)S(1)}, s32[8,512]{1,0:T(8,128)}, u32[]{:S(2)}) copy-start(s32[8,512]{1,0:T(8,128)} %param.6) | copy-start | bytes 49156
  48.7 10.7 %copy-start.2 = (f32[8,518,768]{2,1,0:T(8,128)}, f32[8,518,768]{2,1,0:T(8,128)S(1)}, u32[]{:S(2)}) copy-start(f32[8,518,768]{2,1,0:T(8,128)S(1)} %fusion.22) | copy-start | bytes 38191108
  104.1 10.4 %copy-start.4 = (f32[8,512,768]{2,1,0:T(8,128)S(1)}, f32[8,512,768]{2,1,0:T(8,128)}, u32[]{:S(2)}) copy-start(f32[8,512,768]{2,1,0:T(8,128)} %get-tuple-element.22) | copy-start | bytes 37748740
  114.4 17.0 %slice-start = ((s8[12779520]{0:T(1024)(128)(4,1)}), s8[4194304]{0:T(1024)(128)(4,1)S(1)}, s32[]{:S(2)}) async-start(s8[12779520]{0:T(1024)(128)(4,1)} %bitcast.53), calls=%async_computation.1 | async-start | bytes 8388608
  120.3 11.1 %slice-start.1 = ((s8[12779520]{0:T(1024)(128)(4,1)}), s8[4194304]{0:T(1024)(128)(4,1)S(1)}, s32[]{:S(2)}) async-start(s8[12779520]{0:T(1024)(128)(4,1)} %bitcast.53), calls=%async_computation.2 | async-start | bytes 8388608
  120.3 11.1 %slice-start.2 = ((s8[12779520]{0:T(1024)(128)(4,1)}), s8[4194304]{0:T(1024)(128)(4,1)S(1)}, s32[]{:S(2)}) async-start(s8[12779520]{0:T(1024)(128)(4,1)} %bitcast.53), calls=%async_computation.3 | async-start | bytes 8388608
  120.3 11.1 %slice-start.3 = ((s8[12779520]{0:T(1024)(128)(4,1)}), s8[196608]{0:T(1024)(128)(4,1)S(1)}, s32[]{:S(2)}) async-start(s8[12779520]{0:T(1024)(128)(4,1)} %bitcast.53), calls=%async_computation.4 | async-start | bytes 393216
  228.3 4.6 copy-start.3
  234.1 32.5 %slice-start.4 = ((s8[12779520]{0:T(1024)(128)(4,1)}), s8[4194304]{0:T(1024)(128)(4,1)S(1)}, s32[]{:S(2)}) async-start(s8[12779520]{0:T(1024)(128)(4,1)} %bitcast.55), calls=%async_computation.5 | async-start | bytes 8388608
  234.1 32.5 %slice-start.5 = ((s8[12779520]{0:T(1024)(128)(4,1)}), s8[4194304]{0:T(1024)(128)(4,1)S(1)}, s32[]{:S(2)}) async-start(s8[12779520]{0:T(1024)(128)(4,1)} %bitcast.55), calls=%async_computation.6 | async-start | bytes 8388608
  234.1 32.5 %slice-start.6 = ((s8[12779520]{0:T(1024)(128)(4,1)}), s8[196608]{0:T(1024)(128)(4,1)S(1)}, s32[]{:S(2)}) async-start(s8[12779520]{0:T(1024)(128)(4,1)} %bitcast.55), calls=%async_computation.7 | async-start | bytes 393216
  256.7 9.9 %slice-start.7 = ((s8[12779520]{0:T(1024)(128)(4,1)}), s8[4194304]{0:T(1024)(128)(4,1)S(1)}, s32[]{:S(2)}) async-start(s8[12779520]{0:T(1024)(128)(4,1)} %bitcast.55), calls=%async_computation.8 | async-start | bytes 8388608
  266.6 16.2 %slice-start.8 = ((s8[12582912]{0:T(1024)(128)(4,1)}), s8[4194304]{0:T(1024)(128)(4,1)S(1)}, s32[]{:S(2)}) async-start(s8[12582912]{0:T(1024)(128)(4,1)} %bitcast.57), calls=%async_computation.9 | async-start | bytes 8388608
  266.6 16.2 %slice-start.9 = ((s8[12582912]{0:T(1024)(128)(4,1)}), s8[4194304]{0:T(1024)(128)(4,1)S(1)}, s32[]{:S(2)}) async-start(s8[12582912]{0:T(1024)(128)(4,1)} %bitcast.57), calls=%async_computation.10 | async-start | bytes 8388608
  273.4 9.5 %slice-start.10 = ((s8[12582912]{0:T(1024)(128)(4,1)}), s8[4194304]{0:T(1024)(128)(4,1)S(1)}, s32[]{:S(2)}) async-start(s8[12582912]{0:T(1024)(128)(4,1)} %bitcast.57), calls=%async_computation.11 | async-start | bytes 8388608
  288.8 88.0 %collective-permute-start.2 = (f32[8,6,768]{2,1,0:T(8,128)S(1)}, f32[8,6,768]{2,1,0:T(8,128)S(1)}, u32[]{:S(2)}, u32[]{:S(2)}) collective-permute-start(f32[8,6,768]{2,1,0:T(8,128)S(1)} %pad_add_fusion.2), channel_id=1, source_target_pairs={{1,0},{2,1},{3,2},{5,4},{6,5},{7,6},{9,8},{10,9},{11,10},{13,12},{... | collective-permute-start | bytes 442376 | tf_op jit(solution)/shard_map/ppermute | solution.py:10
  376.8 1.8 copy-start.5
  376.8 147.5 %copy-start.1 = (bf16[256,768]{1,0:T(8,128)(2,1)S(1)}, bf16[256,768]{1,0:T(8,128)(2,1)}, u32[]{:S(2)}) copy-start(bf16[256,768]{1,0:T(8,128)(2,1)} %param.8) | copy-start | bytes 1179652
Sparse Core Ops, SparseCore 0:
  391.1 131.5 all-reduce.10
where the time goes:
time: 542 us; the launch traced here: 531 us
  other arithmetic  199 us (37%)
  waiting for transfers between devices  127 us (23%)
  matrix products  83.1 us (15%)
  local copies, waits for them, and re-layouts  56.7 us (10%)
  blocking collectives  41.5 us (8%)
  between operations  14.7 us (3%)
  starting transfers between devices  9.58 us (2%)
    psum x1, waiting for transfers between devices, per_device(): totals = lax.psum((grad_table, grad_weight, grad_scorer), ('rows', 'seq'))  127 us
    reduce_sum x1, other arithmetic, per_device(): jnp.sum(masked_grad * embedded[:, reach - offset:reach - offset + span],...  41.9 us
    psum x1, blocking collectives, per_device(): totals = lax.psum((grad_table, grad_weight, grad_scorer), ('rows', 'seq'))  41.5 us
    dot_general x4, matrix products, per_device(): jnp.einsum('rcd,d->rc', level, scorer32, precision=lax.Precision.HIGHEST)  36.1 us
    reduce_sum x1, other arithmetic, per_device(): jnp.sum(grad_mixed * level, axis=-1)  35.6 us
    dot_general x4, matrix products, per_device(): jnp.einsum('rc,rcd->d', grad_score[level], pooled[level], precision=lax.P...  32 us
    add x1, other arithmetic, per_device(): grad_embedded + pad_positions(weights32[offset] * masked_grad, reach - of...  22.6 us
    mul x1, other arithmetic, per_device(): pool_masks[offset][:, :, None] * carried  20 us
  transfers between devices with their start and end apart: 4, of which 1 were waited for; matrix products, arithmetic and copies ran while one was open for 15% of the time, Pallas kernels for 0%

commit v1 on v0

v1 whole, which is shorter than its diff:
```python
import functools

import jax
import jax.numpy as jnp
from jax import lax
from jax.experimental import pallas as pl
from jax.experimental.pallas import tpu as pltpu
from jax.sharding import PartitionSpec as P

TAPS = 4
REACH = 5
SPAN = 8
LANES = 128
F32 = jnp.float32
BF16 = jnp.bfloat16
NT = (((1,), (1,)), ((), ()))


def split(x):
    hi = x.astype(BF16)
    return hi, (x - hi.astype(F32)).astype(BF16)


def dot(a, b):
    return jnp.dot(a, b, preferred_element_type=F32)


def dot_nt(a, b):
    return lax.dot_general(a, b, NT, preferred_element_type=F32)


def lanes_of(width):
    step = min(width, LANES)
    return [pl.ds(at, step) for at in range(0, width, step)]


def response_kernel(table_ref, weight_ref, scorer_ref, cot_ref, resp_ref, score_ref, table_t_ref, weight_b_ref, taps):
    vocab, width = table_ref.shape

    @pl.when(pl.program_id(0) == 0)
    def _():
        table = table_ref[...].astype(F32)
        weight = weight_ref[...].astype(F32)
        for k in range(TAPS):
            hi, lo = split(weight[k : k + 1] * table)
            taps[pl.ds(k * vocab, vocab), pl.ds(0, width)] = hi
            taps[pl.ds(k * vocab, vocab), pl.ds(width, width)] = lo
            weight_b_ref[k] = jnp.transpose(jnp.broadcast_to(weight[k : k + 1], (LANES, width)))
        hi, lo = split(weight * scorer_ref[...].astype(F32))
        score_ref[...] = dot_nt(hi, table_ref[...]) + dot_nt(lo, table_ref[...])
        table_t_ref[...] = jnp.transpose(table).astype(BF16)

    cot = cot_ref[0]
    resp_ref[0] = dot_nt(taps[...], jnp.concatenate([cot, cot], axis=1))


def response(table, conv_weight, scorer, cotangent):
    rows, pairs, width = cotangent.shape
    vocab = table.shape[0]
    whole = lambda shape: pl.BlockSpec(shape, lambda i: (0,) * len(shape))
    return pl.pallas_call(
        response_kernel,
        grid=(rows,),
        in_specs=[
            whole((vocab, width)),
            whole((TAPS, width)),
            whole((1, width)),
            pl.BlockSpec((1, pairs, width), lambda i: (i, 0, 0)),
        ],
        out_specs=[
            pl.BlockSpec((1, TAPS * vocab, pairs), lambda i: (i, 0, 0)),
            whole((TAPS, vocab)),
            whole((width, vocab)),
            whole((TAPS, width, LANES)),
        ],
        out_shape=[
            jax.ShapeDtypeStruct((rows, TAPS * vocab, pairs), F32),
            jax.ShapeDtypeStruct((TAPS, vocab), F32),
            jax.ShapeDtypeStruct((width, vocab), BF16),
            jax.ShapeDtypeStruct((TAPS, width, LANES), F32),
        ],
        scratch_shapes=[pltpu.VMEM((TAPS * vocab, 2 * width), BF16)],
        name="response",
    )(table, conv_weight, scorer[None], cotangent)


def look_up(rows_of, index):
    parts = []
    for at in range(0, index.shape[1], LANES):
        part = index[:, at : at + LANES]
        low = part & (LANES - 1)
        take = lambda h: jnp.take_along_axis(
            jnp.broadcast_to(rows_of[h], part.shape), low, axis=1, mode="promise_in_bounds"
        )
        parts.append(jnp.where(part < LANES, take(0), take(1)))
    return jnp.concatenate(parts, axis=1) if len(parts) > 1 else parts[0]


def gradient_kernel(
    code_ref, table_ref, weight_ref, scorer_ref, score_ref, cot_ref, resp_ref,
    mix_ref, table_grad_ref, rest_ref,
    byte_scr, pick_scr, seg_scr, prob_scr, gam_scr, look_scr, eta_scr, sum_scr,
):
    rows, padded = byte_scr.shape[1:]
    vocab, width = table_ref.shape
    pairs = cot_ref.shape[1]
    row = pl.program_id(0)
    tiles = lanes_of(pairs)

    def same(r, k):
        return jnp.where(seg_scr[r] == seg_scr[r + k], 1.0, 0.0)

    def counts(start):
        keep = [same(start, k) for k in range(TAPS)]
        total, inverse = keep[0], []
        for b in range(TAPS):
            if b:
                total = total + keep[b]
            inverse.append(1.0 / total)
        return keep, inverse

    @pl.when(row == 0)
    def _():
        codes = code_ref[...].astype(F32).astype(BF16)
        reach = codes.shape[1]
        halo = reach - 2 * pairs
        at = lax.broadcasted_iota(jnp.int32, (reach, padded), 0)
        pair = lax.broadcasted_iota(jnp.int32, (reach, padded), 1)
        shift = at - 2 * pair - (halo + 1)
        for s in range(SPAN):
            pick = jnp.where(shift == -s, 1.0, 0.0).astype(BF16)
            found = dot(codes, pick)
            byte_scr[s] = found[:rows].astype(jnp.int32)
            seg_scr[s] = found[rows:]
        scored = []
        tables = [[score_ref[k : k + 1, h * LANES : (h + 1) * LANES] for h in range(2)] for k in range(TAPS)]
        for r in range(REACH):
            scored.append(sum(same(r, k) * look_up(tables[k], byte_scr[r + k]) for k in range(TAPS)))
        beta = [0.0] * REACH
        for start in range(2):
            keep, inverse = counts(start)
            running, level = 0.0, []
            for b in range(TAPS):
                running = running + keep[b] * scored[start + b]
                level.append(running * inverse[b])
            top = functools.reduce(jnp.maximum, level)
            level = [jnp.exp(x - top) for x in level]
            norm = 1.0 / sum(level)
            level = [x * norm for x in level]
            share = 0.0
            for b in range(TAPS - 1, -1, -1):
                prob_scr[start * TAPS + b] = level[b]
                share = share + level[b] * inverse[b]
                beta[start + b] = beta[start + b] + 0.5 * keep[b] * share
        for r in range(REACH):
            for k in range(TAPS):
                gam = beta[r] * same(r, k)
                for i in range(rows):
                    gam_scr[i, pl.ds(r * TAPS + k, 1)] = gam[i : i + 1]
        for s in range(SPAN):
            for i in range(rows):
                pick_scr[i, pl.ds(s, 1)] = byte_scr[s, i : i + 1]

    for lane in tiles:
        size = lane.size
        byte = [pick_scr[row, pl.ds(s, 1), lane] for s in range(SPAN)]
        base = lax.broadcasted_iota(jnp.int32, (8, size), 0)
        found = [[jnp.zeros((8, size), F32) for _ in range(TAPS)] for _ in range(REACH)]
        for v in range(0, vocab, 8):
            hit = [b == base + v for b in byte]
            for k in range(TAPS):
                value = resp_ref[0, pl.ds(k * vocab + v, 8), lane]
                for r in range(REACH):
                    found[r][k] = jnp.where(hit[r + k], value, found[r][k])
        for r in range(REACH):
            for k in range(TAPS):
                look_scr[row, pl.ds(r * TAPS + k, 1), lane] = jnp.sum(found[r][k], axis=0, keepdims=True)
    for lane in tiles:
        size = lane.size
        byte = [pick_scr[row, pl.ds(s, 1), lane] for s in range(SPAN)]
        gam = [gam_scr[row, pl.ds(q, 1), lane] for q in range(REACH * TAPS)]
        base = lax.broadcasted_iota(jnp.int32, (16, size), 0)
        for v in range(0, vocab, 16):
            hit = [b == base + v for b in byte]
            for k in range(TAPS):
                mixed = sum(jnp.where(hit[r + k], gam[r * TAPS + k], 0.0) for r in range(REACH))
                hi, lo = split(mixed)
                mix_ref[0, k, pl.ds(v, 16), lane] = hi
                mix_ref[0, k, pl.ds(vocab + v, 16), lane] = lo
    cot = cot_ref[0]
    for k in range(TAPS):
        hi, lo = mix_ref[0, k, :vocab], mix_ref[0, k, vocab:]
        if pairs % LANES == 0:
            part = dot(jnp.concatenate([hi, lo], axis=1), jnp.concatenate([cot, cot], axis=0))
        else:
            part = dot(hi, cot) + dot(lo, cot)
        where = pl.ds(k * vocab, vocab)

        @pl.when(row == 0)
        def _():
            sum_scr[where] = part

        @pl.when(row > 0)
        def _():
            sum_scr[where] += part

    @pl.when(row == rows - 1)
    def _():
        eta = [0.0] * REACH
        products = [sum(same(r, k) * look_scr[:, r * TAPS + k] for k in range(TAPS)) for r in range(REACH)]
        for start in range(2):
            keep, inverse = counts(start)
            prob = [prob_scr[start * TAPS + b] for b in range(TAPS)]
            running, grad = 0.0, []
            for b in range(TAPS):
                running = running + keep[b] * products[start + b]
                grad.append(0.5 * running * inverse[b])
            mean = sum(p * g for p, g in zip(prob, grad))
            share = 0.0
            for b in range(TAPS - 1, -1, -1):
                share = share + prob[b] * (grad[b] - mean) * inverse[b]
                eta[start + b] = eta[start + b] + keep[b] * share
        eta_scr[...] = jnp.zeros_like(eta_scr)
        for r in range(REACH):
            for k in range(TAPS):
                value = eta[r] * same(r, k)
                hi = value.astype(BF16).astype(F32)
                lo = value - hi
                for i in range(rows):
                    eta_scr[i, r + k, k : k + 1] = hi[i : i + 1]
                    eta_scr[i, r + k, TAPS + k : TAPS + k + 1] = lo[i : i + 1]
        base = lax.broadcasted_iota(jnp.int32, (vocab, pairs), 0)

        def scatter(i, total):
            for s in range(SPAN):
                hot = jnp.where(pick_scr[i, pl.ds(s, 1), pl.ds(0, pairs)] == base, 1.0, 0.0).astype(BF16)
                total = total + dot_nt(hot, eta_scr[i, s, :, pl.ds(0, pairs)].astype(BF16))
            return total

        spread = lax.fori_loop(0, rows, scatter, jnp.zeros((vocab, 2 * TAPS), F32))
        spread = spread[:, :TAPS] + spread[:, TAPS:]
        table = table_ref[...].astype(F32)
        weight = weight_ref[...].astype(F32)
        scorer = scorer_ref[...].astype(F32)
        grad, score_grad, conv = 0.0, 0.0, []
        for k in range(TAPS):
            column = spread[:, k : k + 1]
            total = sum_scr[pl.ds(k * vocab, vocab)] + column * scorer
            grad = grad + weight[k : k + 1] * total
            conv.append(jnp.sum(table * total, axis=0, keepdims=True))
            score_grad = score_grad + weight[k : k + 1] * jnp.sum(table * column, axis=0, keepdims=True)
        table_grad_ref[...] = grad
        rest_ref[...] = jnp.concatenate(conv + [score_grad, jnp.zeros((8 - TAPS - 1, width), F32)], axis=0)


def gradient(codes, table, conv_weight, scorer, scores, cotangent, resp):
    rows, pairs, width = cotangent.shape
    vocab = table.shape[0]
    padded = -(-pairs // LANES) * LANES
    whole = lambda shape: pl.BlockSpec(shape, lambda i: (0,) * len(shape))
    return pl.pallas_call(
        gradient_kernel,
        grid=(rows,),
        in_specs=[
            whole(codes.shape),
            whole((vocab, width)),
            whole((TAPS, width)),
            whole((1, width)),
            whole((TAPS, vocab)),
            pl.BlockSpec((1, pairs, width), lambda i: (i, 0, 0)),
            pl.BlockSpec((1, TAPS * vocab, pairs), lambda i: (i, 0, 0)),
        ],
        out_specs=[
            pl.BlockSpec((1, TAPS, 2 * vocab, pairs), lambda i: (i, 0, 0, 0)),
            whole((vocab, width)),
            whole((8, width)),
        ],
        out_shape=[
            jax.ShapeDtypeStruct((rows, TAPS, 2 * vocab, pairs), BF16),
            jax.ShapeDtypeStruct((vocab, width), F32),
            jax.ShapeDtypeStruct((8, width), F32),
        ],
        scratch_shapes=[
            pltpu.VMEM((SPAN, rows, padded), jnp.int32),
            pltpu.VMEM((rows, SPAN, padded), jnp.int32),
            pltpu.VMEM((SPAN, rows, padded), F32),
            pltpu.VMEM((2 * TAPS, rows, padded), F32),
            pltpu.VMEM((rows, REACH * TAPS, padded), F32),
            pltpu.VMEM((rows, REACH * TAPS, padded), F32),
            pltpu.VMEM((rows, SPAN, 2 * TAPS, padded), F32),
            pltpu.VMEM((TAPS * vocab, width), F32),
        ],
        name="gradient",
    )(codes, table, conv_weight, scorer[None], scores, cotangent, resp)


def blocks_kernel(table_t_ref, weight_b_ref, mix_ref, out_ref):
    width = table_t_ref.shape[0]
    pairs = out_ref.shape[1]
    step = 256
    for d in range(0, width, step):
        table_t = table_t_ref[pl.ds(d, step)]
        both = jnp.concatenate([table_t, table_t], axis=1)
        total = 0.0
        for k in range(TAPS):
            weight = weight_b_ref[k, pl.ds(d, step)]
            if pairs > LANES:
                weight = jnp.concatenate([weight] * (pairs // LANES), axis=1)
            else:
                weight = weight[:, :pairs]
            total = total + weight * dot(both, mix_ref[0, k])
        out_ref[0, :, pl.ds(d, step)] = jnp.transpose(total).astype(BF16)


def blocks(table_t, weight_b, mix):
    rows, _, _, pairs = mix.shape
    width, vocab = table_t.shape
    whole = lambda shape: pl.BlockSpec(shape, lambda i: (0,) * len(shape))
    return pl.pallas_call(
        blocks_kernel,
        grid=(rows,),
        in_specs=[
            whole((width, vocab)),
            whole(weight_b.shape),
            pl.BlockSpec((1,) + mix.shape[1:], lambda i: (i, 0, 0, 0)),
        ],
        out_specs=pl.BlockSpec((1, pairs, width), lambda i: (i, 0, 0)),
        out_shape=jax.ShapeDtypeStruct((rows, pairs, width), BF16),
        name="blocks",
    )(table_t, weight_b, mix)


def reduce_all(table_grad, rest, rows_axis, seq_axis):
    ranks, parts = lax.axis_size(rows_axis), lax.axis_size(seq_axis)
    rank, part = lax.axis_index(rows_axis), lax.axis_index(seq_axis)

    def swap(x, axis, stride):
        return lax.ppermute(x, axis, [(i, i ^ stride) for i in range(lax.axis_size(axis))])

    vocab, width = table_grad.shape
    half = width // 2
    core = rank % 2
    whole = jnp.concatenate([table_grad, rest], axis=0)
    mine = lax.dynamic_slice_in_dim(whole, core * half, half, 1)
    other = lax.dynamic_slice_in_dim(whole, (1 - core) * half, half, 1)
    mine = mine + swap(other, rows_axis, 1)
    grad, rest = mine[:vocab], mine[vocab:]
    stride = parts // 2
    while stride:
        size = grad.shape[0] // 2
        bit = (part // stride) % 2
        sent = jnp.concatenate([lax.dynamic_slice_in_dim(grad, (1 - bit) * size, size, 0), rest], axis=0)
        kept = jnp.concatenate([lax.dynamic_slice_in_dim(grad, bit * size, size, 0), rest], axis=0)
        got = kept + swap(sent, seq_axis, stride)
        grad, rest = got[:size], got[size:]
        stride //= 2
    mine = jnp.concatenate([grad, rest], axis=0)
    stride = 2
    while stride < ranks:
        mine = mine + swap(mine, rows_axis, stride)
        stride *= 2
    other = swap(mine, rows_axis, 1)
    both = jnp.where(
        core == 0, jnp.concatenate([mine, other], axis=1), jnp.concatenate([other, mine], axis=1)
    )
    share = vocab // parts
    return both[:share], both[share : share + TAPS], both[share + TAPS]


def per_device(byte_ids, segment_ids, table, conv_weight, scorer, cotangent):
    parts = lax.axis_size("seq")
    codes = jnp.concatenate([byte_ids, segment_ids], axis=0)
    tail = codes[:, -LANES:]
    halo = lax.ppermute(tail, "seq", [(i, i + 1) for i in range(parts - 1)])
    halo = jnp.where(lax.axis_index("seq") == 0, -1, halo)
    resp, scores, table_t, weight_b = response(table, conv_weight, scorer, cotangent)
    codes = jnp.concatenate([halo, codes], axis=1)
    mix, table_grad, rest = gradient(codes, table, conv_weight, scorer, scores, cotangent, resp)
    blocks_out = blocks(table_t, weight_b, mix)
    table_grad, conv_grad, scorer_grad = reduce_all(table_grad, rest, "rows", "seq")
    return (blocks_out, table_grad, conv_grad, scorer_grad)


def solution(mesh):
    return jax.shard_map(
        per_device,
        mesh=mesh,
        in_specs=(P("rows", "seq"), P("rows", "seq"), P(), P(), P(), P("rows", "seq", None)),
        out_specs=(P("rows", "seq", None), P("seq", None), P(), P()),
        check_vma=False,
    )
```

time: 542 us -> 95.3 us (0.18); the launches traced: 531 us -> 94.5 us
  other arithmetic: 199 us -> 0.81 us
  waiting for transfers between devices: 127 us -> 17.8 us
  matrix products: 83.1 us -> 0 us
  Pallas kernels: 0 us -> 55.7 us
  local copies, waits for them, and re-layouts: 56.7 us -> 6.67 us
  blocking collectives: 41.5 us -> 0 us
  between operations: 14.7 us -> 0.8 us
    psum x1 -> x0, waiting for transfers between devices: 127 us -> none  [per_device(): totals = lax.psum((grad_table, grad_weight, grad_scorer), ('rows', 'seq'))]
    reduce_sum x5 -> x0, other arithmetic: 97.1 us -> none  [the longest x1 41.9 us: per_device(): jnp.sum(masked_grad * embedded[:, reach - offset:reach - offset + span],...]
    dot_general x10 -> x0, matrix products: 83.1 us -> none  [the longest x4 36.1 us: per_device(): jnp.einsum('rcd,d->rc', level, scorer32, precision=lax.Precision.HIGHEST)]
    pallas_call x0 -> x3, Pallas kernels: none -> 55.7 us  [the longest x1 31.2 us: gradient(): pl.pallas_call(gradient_kernel, grid=(rows,), in_specs=[whole(codes.shape...]
    add x7 -> x5, other arithmetic: 53.1 us -> 0.13 us  [the longest x1 0.06 us: reduce_all(): mine = mine + swap(other, rows_axis, 1)]
    psum x1 -> x0, blocking collectives: 41.5 us -> none  [per_device(): totals = lax.psum((grad_table, grad_weight, grad_scorer), ('rows', 'seq'))]
    mul x4 -> x0, other arithmetic: 39.4 us -> none  [the longest x1 20 us: per_device(): pool_masks[offset][:, :, None] * carried]
    reshape x2 -> x0, local copies, waits for them, and re-layouts: 30.9 us -> none  [the longest x1 15.8 us: per_device(): grad_mixed = jnp.repeat(0.5 * cotangent.astype(jnp.float32), 2, axis=1)]
  transfers between devices with their start and end apart: 4 -> 7, of which waited for: 1 -> 5; matrix products, arithmetic and copies ran while one was open for 15% -> 1% of each run, Pallas kernels for 0% -> 26%
where the time goes in v1:
time: 95.3 us; the launch traced here: 94.5 us
  Pallas kernels  55.7 us (58%)
  waiting for transfers between devices  17.8 us (19%)
  starting transfers between devices  12.8 us (13%)
  local copies, waits for them, and re-layouts  6.67 us (7%)
    pallas_call x1, Pallas kernels, gradient(): pl.pallas_call(gradient_kernel, grid=(rows,), in_specs=[whole(codes.shape...  31.2 us
    ppermute x6, waiting for transfers between devices, swap(): lax.ppermute(x, axis, [(i, i ^ stride) for i in range(lax.axis_size(axis))])  17.8 us
    pallas_call x1, Pallas kernels, blocks(): pl.pallas_call(blocks_kernel, grid=(rows,), in_specs=[whole((width, vocab...  12.2 us
    pallas_call x1, Pallas kernels, response(): pl.pallas_call(response_kernel, grid=(rows,), in_specs=[whole((vocab, wid...  12.2 us
    ppermute x6, starting transfers between devices, swap(): lax.ppermute(x, axis, [(i, i ^ stride) for i in range(lax.axis_size(axis))])  7.94 us
    ppermute x1, starting transfers between devices, per_device(): halo = lax.ppermute(tail, 'seq', [(i, i + 1) for i in range(parts - 1)])  4.86 us
    unnamed x2, local copies, waits for them, and re-layouts  1.91 us
  transfers between devices with their start and end apart: 7, of which 5 were waited for; matrix products, arithmetic and copies ran while one was open for 1% of the time, Pallas kernels for 26%

profile of v1, /device:TPU:0, one launch (start us, length us, event | category | flops | bytes accessed | tf_op | source)
XLA Modules:
  0.0 94.5 jit_solution(515061465183439804)
XLA Ops:
  0.6 0.7 constant_dynamic-update-slice_fusion.1
  1.4 0.7 constant_dynamic-update-slice_fusion
  2.1 4.9 %collective-permute-start = (s32[16,128]{1,0:T(8,128)S(1)}, s32[16,128]{1,0:T(8,128)S(1)}, u32[]{:S(2)}, u32[]{:S(2)}) collective-permute-start(s32[16,128]{1,0:T(8,128)S(1)} %slice.35), channel_id=1, source_target_pairs={{0,1},{1,2},{2,3},{4,5},{5,6},{6,7},{8,9},{9,10},{10,11},{12,13},{... | collective-permute-start | bytes 24584 | tf_op jit(solution)/shard_map/ppermute | solution.py:374
  7.0 1.3 %broadcast_in_dim.8.scorer_ref = bf16[1,768]{1,0:T(2,128)(2,1)} reshape(bf16[768]{0:T(1024)(128)(2,1)} %param.10) | data formatting | bytes 3072 | tf_op jit(solution)/shard_map/broadcast_in_dim | solution.py:84
  8.2 12.2 %response.1 = (f32[8,1024,256]{2,1,0:T(8,128)}, f32[4,256]{1,0:T(4,128)}, bf16[768,256]{1,0:T(8,128)(2,1)}, f32[4,768,128]{2,1,0:T(8,128)}) custom-call(bf16[256,768]{1,0:T(8,128)(2,1)} %table_ref.3, bf16[4,768]{1,0:T(4,128)(2,1)} %weight_ref.3, bf16[1,768]{1,0:T(2,128)(2,1)} %broadcast_in_dim.8.scorer_ref, bf16[8,256,768]{2,1,0:T(8,128)(2,1)} %cot_ref.3), custom_call_target="tpu_custom_call" | custom-call | tf_op jit(solution)/shard_map/response/pallas_call | solution.py:61
  20.4 0.0 collective-permute-done
  20.4 0.6 pad_add_fusion.code_ref
  21.1 31.2 %gradient.1 = (bf16[8,4,512,256]{3,2,1,0:T(8,128)(2,1)}, f32[256,768]{1,0:T(8,128)}, f32[8,768]{1,0:T(8,128)}) custom-call(s32[16,640]{1,0:T(8,128)} %pad_add_fusion.code_ref, bf16[256,768]{1,0:T(8,128)(2,1)} %table_ref.3, bf16[4,768]{1,0:T(4,128)(2,1)} %weight_ref.3, bf16[1,768]{1,0:T(2,128)(2,1)} %broadcast_in_dim.8.scorer_ref, ...), custom_call_target="tpu_custom_call" | custom-call | tf_op jit(solution)/shard_map/gradient/pallas_call | solution.py:261
  52.3 1.2 %constant_dynamic-update-slice_fusion.3 = f32[264,768]{1,0:T(8,128)S(1)} fusion(f32[256,768]{1,0:T(8,128)} %get-tuple-element.16), kind=kLoop, calls=%fused_computation.12 | loop fusion | bytes 1572864
  53.5 0.7 constant_dynamic-update-slice_fusion.2
  54.2 0.1 collective-permute-start.1
  54.4 1.7 %collective-permute-done.1 = f32[264,384]{1,0:T(8,128)S(1)} collective-permute-done((f32[264,384]{1,0:T(8,128)S(1)}, f32[264,384]{1,0:T(8,128)S(1)}, u32[]{:S(2)}, u32[]{:S(2)}) %collective-permute-start.1) | collective-permute-done | bytes 405536 | tf_op jit(solution)/shard_map/ppermute | solution.py:338
  56.0 0.1 dynamic-slice_add_fusion
  56.2 1.6 %collective-permute-start.2 = (f32[136,384]{1,0:T(8,128)S(1)}, f32[136,384]{1,0:T(8,128)S(1)}, u32[]{:S(2)}, u32[]{:S(2)}) collective-permute-start(f32[136,384]{1,0:T(8,128)S(1)} %pad_maximum_fusion), channel_id=1, source_target_pairs={{0,2},{1,3},{2,0},{3,1},{4,6},{5,7},{6,4},{7,5},{8,10},{9,11},{10,... | collective-permute-start | bytes 626696 | tf_op jit(solution)/shard_map/ppermute | solution.py:338
  57.8 5.7 %collective-permute-done.2 = f32[136,384]{1,0:T(8,128)S(1)} collective-permute-done((f32[136,384]{1,0:T(8,128)S(1)}, f32[136,384]{1,0:T(8,128)S(1)}, u32[]{:S(2)}, u32[]{:S(2)}) %collective-permute-start.2) | collective-permute-done | bytes 208928 | tf_op jit(solution)/shard_map/ppermute | solution.py:338
  63.6 1.5 %collective-permute-start.3 = (f32[72,384]{1,0:T(8,128)S(1)}, f32[72,384]{1,0:T(8,128)S(1)}, u32[]{:S(2)}, u32[]{:S(2)}) collective-permute-start(f32[72,384]{1,0:T(8,128)S(1)} %pad_maximum_fusion.2), channel_id=1, source_target_pairs={{0,1},{1,0},{2,3},{3,2},{4,5},{5,4},{6,7},{7,6},{8,9},{9,8},{10,11... | collective-permute-start | bytes 331784 | tf_op jit(solution)/shard_map/ppermute | solution.py:338
  65.1 3.3 %collective-permute-done.3 = f32[72,384]{1,0:T(8,128)S(1)} collective-permute-done((f32[72,384]{1,0:T(8,128)S(1)}, f32[72,384]{1,0:T(8,128)S(1)}, u32[]{:S(2)}, u32[]{:S(2)}) %collective-permute-start.3) | collective-permute-done | bytes 110624 | tf_op jit(solution)/shard_map/ppermute | solution.py:338
  68.4 1.6 %collective-permute-start.4 = (f32[72,384]{1,0:T(8,128)S(1)}, f32[72,384]{1,0:T(8,128)S(1)}, u32[]{:S(2)}, u32[]{:S(2)}) collective-permute-start(f32[72,384]{1,0:T(8,128)S(1)} %fusion.1), channel_id=1, source_target_pairs={{0,8},{4,12},{8,0},{12,4},{16,24},{20,28},{24,16},{28,20},{1,9},{5... | collective-permute-start | bytes 331784 | tf_op jit(solution)/shard_map/ppermute | solution.py:338
  70.1 3.2 %collective-permute-done.4 = f32[72,384]{1,0:T(8,128)S(1)} collective-permute-done((f32[72,384]{1,0:T(8,128)S(1)}, f32[72,384]{1,0:T(8,128)S(1)}, u32[]{:S(2)}, u32[]{:S(2)}) %collective-permute-start.4) | collective-permute-done | bytes 110624 | tf_op jit(solution)/shard_map/ppermute | solution.py:338
  73.3 3.1 %collective-permute-start.5 = (f32[72,384]{1,0:T(8,128)S(1)}, f32[72,384]{1,0:T(8,128)S(1)}, u32[]{:S(2)}, u32[]{:S(2)}) collective-permute-start(f32[72,384]{1,0:T(8,128)S(1)} %add.57), channel_id=1, source_target_pairs={{0,16},{4,20},{8,24},{12,28},{16,0},{20,4},{24,8},{28,12},{1,17},{... | collective-permute-start | bytes 331784 | tf_op jit(solution)/shard_map/ppermute | solution.py:338
  76.3 3.9 %collective-permute-done.5 = f32[72,384]{1,0:T(8,128)S(1)} collective-permute-done((f32[72,384]{1,0:T(8,128)S(1)}, f32[72,384]{1,0:T(8,128)S(1)}, u32[]{:S(2)}, u32[]{:S(2)}) %collective-permute-start.5) | collective-permute-done | bytes 110624 | tf_op jit(solution)/shard_map/ppermute | solution.py:338
  80.2 0.1 collective-permute-start.6
  80.3 12.2 %blocks.1 = bf16[8,256,768]{2,1,0:T(8,128)(2,1)} custom-call(bf16[768,256]{1,0:T(8,128)(2,1)} %get-tuple-element.11.table_t_ref, f32[4,768,128]{2,1,0:T(8,128)} %get-tuple-element.12.weight_b_ref, bf16[8,4,512,256]{3,2,1,0:T(8,128)(2,1)} %get-tuple-element.15.mix_ref), custom_call_target="tpu_custom_call" | custom-call | tf_op jit(solution)/shard_map/blocks/pallas_call | solution.py:319
  92.6 0.0 collective-permute-done.6
  92.6 0.7 slice.40
  93.3 0.6 slice.41
  93.9 0.6 slice_reduce_fusion
  (16 shorter events, 0.3 us)
Async XLA Ops:
  2.1 18.4 %collective-permute-start = (s32[16,128]{1,0:T(8,128)S(1)}, s32[16,128]{1,0:T(8,128)S(1)}, u32[]{:S(2)}, u32[]{:S(2)}) collective-permute-start(s32[16,128]{1,0:T(8,128)S(1)} %slice.35), channel_id=1, source_target_pairs={{0,1},{1,2},{2,3},{4,5},{5,6},{6,7},{8,9},{9,10},{10,11},{12,13},{... | collective-permute-start | bytes 24584 | tf_op jit(solution)/shard_map/ppermute | solution.py:374
  54.2 1.8 %collective-permute-start.1 = (f32[264,384]{1,0:T(8,128)S(1)}, f32[264,384]{1,0:T(8,128)S(1)}, u32[]{:S(2)}, u32[]{:S(2)}) collective-permute-start(f32[264,384]{1,0:T(8,128)S(1)} %constant_dynamic-slice_fusion.4), channel_id=1, source_target_pairs={{0,4},{4,0},{8,12},{12,8},{16,20},{20,16},{24,28},{28,24},{1,5},{5... | collective-permute-start | bytes 1216520 | tf_op jit(solution)/shard_map/ppermute | solution.py:338
  56.2 7.3 %collective-permute-start.2 = (f32[136,384]{1,0:T(8,128)S(1)}, f32[136,384]{1,0:T(8,128)S(1)}, u32[]{:S(2)}, u32[]{:S(2)}) collective-permute-start(f32[136,384]{1,0:T(8,128)S(1)} %pad_maximum_fusion), channel_id=1, source_target_pairs={{0,2},{1,3},{2,0},{3,1},{4,6},{5,7},{6,4},{7,5},{8,10},{9,11},{10,... | collective-permute-start | bytes 626696 | tf_op jit(solution)/shard_map/ppermute | solution.py:338
  63.6 4.8 %collective-permute-start.3 = (f32[72,384]{1,0:T(8,128)S(1)}, f32[72,384]{1,0:T(8,128)S(1)}, u32[]{:S(2)}, u32[]{:S(2)}) collective-permute-start(f32[72,384]{1,0:T(8,128)S(1)} %pad_maximum_fusion.2), channel_id=1, source_target_pairs={{0,1},{1,0},{2,3},{3,2},{4,5},{5,4},{6,7},{7,6},{8,9},{9,8},{10,11... | collective-permute-start | bytes 331784 | tf_op jit(solution)/shard_map/ppermute | solution.py:338
  68.4 4.8 %collective-permute-start.4 = (f32[72,384]{1,0:T(8,128)S(1)}, f32[72,384]{1,0:T(8,128)S(1)}, u32[]{:S(2)}, u32[]{:S(2)}) collective-permute-start(f32[72,384]{1,0:T(8,128)S(1)} %fusion.1), channel_id=1, source_target_pairs={{0,8},{4,12},{8,0},{12,4},{16,24},{20,28},{24,16},{28,20},{1,9},{5... | collective-permute-start | bytes 331784 | tf_op jit(solution)/shard_map/ppermute | solution.py:338
  73.3 7.0 %collective-permute-start.5 = (f32[72,384]{1,0:T(8,128)S(1)}, f32[72,384]{1,0:T(8,128)S(1)}, u32[]{:S(2)}, u32[]{:S(2)}) collective-permute-start(f32[72,384]{1,0:T(8,128)S(1)} %add.57), channel_id=1, source_target_pairs={{0,16},{4,20},{8,24},{12,28},{16,0},{20,4},{24,8},{28,12},{1,17},{... | collective-permute-start | bytes 331784 | tf_op jit(solution)/shard_map/ppermute | solution.py:338
  80.2 12.3 %collective-permute-start.6 = (f32[72,384]{1,0:T(8,128)S(1)}, f32[72,384]{1,0:T(8,128)S(1)}, u32[]{:S(2)}, u32[]{:S(2)}) collective-permute-start(f32[72,384]{1,0:T(8,128)S(1)} %add.58), channel_id=1, source_target_pairs={{0,4},{4,0},{8,12},{12,8},{16,20},{20,16},{24,28},{28,24},{1,5},{5... | collective-permute-start | bytes 331784 | tf_op jit(solution)/shard_map/ppermute | solution.py:338

commit v2 on v1

v2 whole, which is shorter than its diff:
```python
import functools

import jax
import jax.numpy as jnp
from jax import lax
from jax.experimental import pallas as pl
from jax.experimental.pallas import tpu as pltpu
from jax.sharding import PartitionSpec as P

TAPS = 4
REACH = 5
SPAN = 8
LANES = 128
F32 = jnp.float32
BF16 = jnp.bfloat16
NT = (((1,), (1,)), ((), ()))


def split(x):
    hi = x.astype(BF16)
    return hi, (x - hi.astype(F32)).astype(BF16)


def dot(a, b):
    return jnp.dot(a, b, preferred_element_type=F32)


def dot_nt(a, b):
    return lax.dot_general(a, b, NT, preferred_element_type=F32)


def lanes_of(width):
    step = min(width, LANES)
    return [pl.ds(at, step) for at in range(0, width, step)]


def score_kernel(table_ref, weight_ref, scorer_ref, score_ref):
    hi, lo = split(weight_ref[...].astype(F32) * scorer_ref[...].astype(F32))
    score_ref[...] = dot_nt(hi, table_ref[...]) + dot_nt(lo, table_ref[...])


def score_table(table, conv_weight, scorer):
    return pl.pallas_call(
        score_kernel,
        out_shape=jax.ShapeDtypeStruct((TAPS, table.shape[0]), F32),
        name="score_table",
    )(table, conv_weight, scorer[None])


def look_up(rows_of, index):
    parts = []
    for at in range(0, index.shape[1], LANES):
        part = index[:, at : at + LANES]
        low = part & (LANES - 1)
        take = lambda h: jnp.take_along_axis(
            jnp.broadcast_to(rows_of[h], part.shape), low, axis=1, mode="promise_in_bounds"
        )
        parts.append(jnp.where(part < LANES, take(0), take(1)))
    return jnp.concatenate(parts, axis=1)


HALO = 16
GROUPS = 4


def main_kernel(
    code_ref, table_ref, weight_ref, scorer_ref, score_ref, cot_ref,
    out_ref, table_grad_ref, rest_ref,
    pick_scr, gam_scr, col_scr, column_scr, keep_scr, prob_scr, rim_scr, emb_a, emb_b, conv_scr, dcol_scr, prod_scr, zeta_scr,
    weight_scr, mix_a, mix_b, sum_scr,
):
    rows, _, padded = pick_scr.shape
    vocab, width = table_ref.shape
    pairs = cot_ref.shape[1]
    row = pl.program_id(0)
    tiles = width // LANES

    def back(x, n):
        return pltpu.roll(x, n % padded, axis=1) if n % padded else x

    def keeps(parity, k):
        return keep_scr[parity * TAPS + k] if k else 1.0

    def same(r, k):
        return back(keep_scr[r % 2 * TAPS + k], r // 2) if k else 1.0

    def counts(start):
        total, inverse = 1.0, [1.0]
        for b in range(1, TAPS):
            total = total + keeps(start, b)
            inverse.append(1.0 / total)
        return inverse

    def put(scr, q, value):
        for i in range(rows):
            scr[i, pl.ds(q, 1)] = value[i : i + 1]

    @pl.when(row == 0)
    def _():
        codes = code_ref[...].astype(F32).astype(BF16)
        reach = codes.shape[1]
        ahead = reach - 2 * pairs
        at = lax.broadcasted_iota(jnp.int32, (reach, padded), 0) - ahead
        lane = lax.broadcasted_iota(jnp.int32, (reach, padded), 1)
        place = at - 2 * jnp.where(lane < pairs, lane, lane - padded)
        byte, seg = [], []
        for parity in range(2):
            found = dot(codes, jnp.where(place == 1 - parity, 1.0, 0.0).astype(BF16))
            byte.append(found[:rows])
            seg.append(found[rows:])
        for parity in range(2):
            put(col_scr, parity, byte[parity])
            for k in range(1, TAPS):
                s = parity + k
                keep = jnp.where(seg[parity] == back(seg[s % 2], s // 2), 1.0, 0.0)
                keep_scr[parity * TAPS + k] = keep
                put(col_scr, 2 + parity * (TAPS - 1) + k - 1, keep)
        byte = [b.astype(jnp.int32) for b in byte]
        for s in range(SPAN):
            put(pick_scr, s, back(byte[s % 2], s // 2))
        found = []
        for k in range(TAPS):
            halves = [score_ref[k : k + 1, h * LANES : (h + 1) * LANES] for h in range(2)]
            found.append([look_up(halves, byte[parity]) for parity in range(2)])
        scored = [
            sum(keeps(parity, k) * back(found[k][(parity + k) % 2], (parity + k) // 2) for k in range(TAPS))
            for parity in range(2)
        ]
        beta = [0.0] * REACH
        for start in range(2):
            inverse = counts(start)
            running, level = 0.0, []
            for b in range(TAPS):
                running = running + keeps(start, b) * back(scored[(start + b) % 2], (start + b) // 2)
                level.append(running * inverse[b])
            top = functools.reduce(jnp.maximum, level)
            level = [jnp.exp(x - top) for x in level]
            norm = 1.0 / sum(level)
            level = [x * norm for x in level]
            share = 0.0
            for b in range(TAPS - 1, -1, -1):
                prob_scr[start * TAPS + b] = level[b]
                share = share + level[b] * inverse[b]
                beta[start + b] = beta[start + b] + 0.5 * keeps(start, b) * share
        for r in range(REACH):
            put(col_scr, 2 * TAPS + r, beta[r])
            for k in range(TAPS):
                put(gam_scr, r * TAPS + k, beta[r] * same(r, k))

    deep = HALO + pairs
    group = pairs // GROUPS
    part_v = vocab // GROUPS

    embs, mixes = (emb_a, emb_b), (mix_a, mix_b)

    def spot(parity, d):
        return (parity * tiles + d) * deep

    def embed(i, slot, j):
        at = pl.multiple_of(HALO + j * group, 8)
        column = column_scr[i, pl.ds(at, group)]
        value = lax.broadcasted_iota(jnp.int32, (group, vocab), 1).astype(F32)
        hot = [jnp.where(column[:, p : p + 1] == value, 1.0, 0.0).astype(BF16) for p in range(2)]
        found = dot(jnp.concatenate(hot, axis=0), table_ref[...])
        for p in range(2):
            for d in range(tiles):
                to = pl.multiple_of(spot(p, d) + at, 8)
                embs[slot][pl.ds(to, group)] = found[p * group : (p + 1) * group, d * LANES : (d + 1) * LANES]

    def embed_rim(i, slot):
        for p in range(2):
            for d in range(tiles):
                to = pl.multiple_of(spot(p, d), 8)
                embs[slot][pl.ds(to, HALO)] = rim_scr[p, d, i]

    def mixing(i, slot, j):
        for lane in lanes_of(pairs):
            size = lane.size
            byte = [pick_scr[i, pl.ds(s, 1), lane] for s in range(SPAN)]
            gam = [gam_scr[i, pl.ds(q, 1), lane] for q in range(REACH * TAPS)]
            base = lax.broadcasted_iota(jnp.int32, (16, size), 0) + j * part_v
            for v in range(0, part_v, 16):
                hit = [b == base + v for b in byte]
                at = pl.ds(pl.multiple_of(j * part_v + v, 16), 16)
                for k in range(TAPS):
                    mixed = sum(jnp.where(hit[r + k], gam[r * TAPS + k], 0.0) for r in range(REACH))
                    hi, lo = split(mixed)
                    mixes[slot][k, 0, at, lane] = hi
                    mixes[slot][k, 1, at, lane] = lo

    def gather(slot, j):
        cot = cot_ref[0]
        at = pl.ds(pl.multiple_of(j * part_v, 16), part_v)
        hi = jnp.concatenate([mixes[slot][k, 0, at] for k in range(TAPS)], axis=0)
        lo = jnp.concatenate([mixes[slot][k, 1, at] for k in range(TAPS)], axis=0)
        if pairs % LANES == 0:
            part = dot(jnp.concatenate([hi, lo], axis=1), jnp.concatenate([cot, cot], axis=0))
        else:
            part = dot(hi, cot) + dot(lo, cot)
        for k in range(TAPS):
            sum_scr[pl.ds(pl.multiple_of(k * vocab + j * part_v, 8), part_v)] += part[k * part_v : (k + 1) * part_v]

    def conved(slot, at, column, d):
        taken = [embs[slot][pl.ds(spot(s % 2, d) + at - s // 2, 8)] for s in range(REACH)]
        for p in range(2):
            total = weight_scr[0, d] * taken[p]
            for k in range(1, TAPS):
                keep = column[:, 2 + p * (TAPS - 1) + k - 1 :][:, :1]
                total = total + keep * (weight_scr[k, d] * taken[p + k])
            conv_scr[pl.ds(pl.multiple_of(spot(p, d) + at, 8), 8)] = total

    lane_at = lax.broadcasted_iota(jnp.int32, (8, LANES), 1) - 8 * row

    def convolve(slot, j):
        for t in range(0, group, 8):
            at = pl.multiple_of(HALO + j * group + t, 8)
            column = column_scr[row, pl.ds(at, 8)]
            for d in range(tiles):
                conved(slot, at, column, d)

    def blocks(j):
        for t in range(0, group, 16):
            start = pl.multiple_of(j * group + t, 16)
            column = [column_scr[row, pl.ds(pl.multiple_of(HALO + start + u, 8), 8)] for u in (0, 8)]
            products = [[0.0] * REACH for _ in range(2)]
            for d in range(tiles):
                lanes = pl.ds(d * LANES, LANES)
                grad = cot_ref[0, pl.ds(start, 16), lanes].astype(F32)
                out = []
                for u in range(2):
                    at = HALO + start + 8 * u
                    mixed = 0.0
                    for r in range(REACH):
                        conv = conv_scr[pl.ds(spot(r % 2, d) + at - r // 2, 8)]
                        products[u][r] = products[u][r] + grad[8 * u : 8 * u + 8] * conv
                        mixed = mixed + column[u][:, 2 * TAPS + r : 2 * TAPS + r + 1] * conv
                    out.append(mixed)
                out_ref[0, pl.ds(start, 16), lanes] = jnp.concatenate(out, axis=0).astype(BF16)
            for u in range(2):
                to = pl.ds(pl.multiple_of(start + 8 * u, 8), 8)
                found = dcol_scr[to]
                for r in range(REACH):
                    found = jnp.where(lane_at == r, jnp.sum(products[u][r], axis=1, keepdims=True), found)
                dcol_scr[to] = found

    @pl.when(row == 0)
    def _():
        for i in range(rows):
            column = jnp.transpose(col_scr[i])
            column_scr[i, pl.ds(0, HALO)] = column[padded - HALO :]
            column_scr[i, pl.ds(HALO, pairs)] = column[:pairs]
        value = lax.broadcasted_iota(jnp.int32, (HALO, vocab), 1).astype(F32)
        for p in range(2):
            hot = [
                jnp.where(column_scr[i, pl.ds(0, HALO)][:, p : p + 1] == value, 1.0, 0.0).astype(BF16)
                for i in range(rows)
            ]
            found = dot(jnp.concatenate(hot, axis=0), table_ref[...])
            for d in range(tiles):
                for i in range(rows):
                    rim_scr[p, d, i] = found[i * HALO : (i + 1) * HALO, d * LANES : (d + 1) * LANES]
        for k in range(TAPS):
            for d in range(tiles):
                lanes = pl.ds(d * LANES, LANES)
                weight_scr[k, d] = jnp.broadcast_to(weight_ref[k : k + 1, lanes].astype(F32), (8, LANES))
        sum_scr[...] = jnp.zeros_like(sum_scr)
        dcol_scr[...] = jnp.zeros_like(dcol_scr)
        embed_rim(0, 0)

        @pl.loop(0, GROUPS)
        def _(j):
            embed(0, 0, j)
            mixing(0, 0, j)

    def work(slot, more):
        if more:
            embed_rim(row + 1, 1 - slot)
        rim = column_scr[row, pl.ds(HALO - 8, 8)]
        for d in range(tiles):
            conved(slot, HALO - 8, rim, d)

        @pl.loop(0, GROUPS)
        def _(j):
            convolve(slot, j)
            gather(slot, j)
            if more:
                mixing(row + 1, 1 - slot, j)
                embed(row + 1, 1 - slot, j)
            blocks(j)

    last = rows - 1
    pl.when((row < last) & (row % 2 == 0))(lambda: work(0, True))
    pl.when((row < last) & (row % 2 == 1))(lambda: work(1, True))
    pl.when(row == last)(lambda: work(last % 2, False))

    @pl.when(row == rows - 1)
    def _():
        inside = lax.broadcasted_iota(jnp.int32, (rows, padded), 1) < pairs
        turned = jnp.transpose(dcol_scr[...])
        for i in range(rows):
            prod_scr[i, :, pl.ds(0, pairs)] = turned[8 * i : 8 * i + 8]
        products = [prod_scr[:, r] for r in range(REACH)]
        eta = [0.0] * REACH
        for start in range(2):
            inverse = counts(start)
            prob = [prob_scr[start * TAPS + b] for b in range(TAPS)]
            running, grad = 0.0, []
            for b in range(TAPS):
                running = running + keeps(start, b) * products[start + b]
                grad.append(0.5 * running * inverse[b])
            mean = sum(p * g for p, g in zip(prob, grad))
            share = 0.0
            for b in range(TAPS - 1, -1, -1):
                share = share + prob[b] * (grad[b] - mean) * inverse[b]
                eta[start + b] = eta[start + b] + keeps(start, b) * share
        eta = [jnp.where(inside, x, 0.0) for x in eta]
        alpha = [sum(back(eta[r], -(r // 2)) for r in range(parity, REACH, 2)) for parity in range(2)]
        for parity in range(2):
            for k in range(TAPS):
                other = (parity + k) % 2
                ahead = (k + 1 - parity) // 2
                hi = back(alpha[other] * keeps(other, k), -ahead)
                low = hi - hi.astype(BF16).astype(F32)
                hi = hi - low
                for i in range(rows):
                    zeta_scr[i, parity, k : k + 1] = hi[i : i + 1]
                    zeta_scr[i, parity, TAPS + k : TAPS + k + 1] = low[i : i + 1]
        base = lax.broadcasted_iota(jnp.int32, (vocab, padded), 0)

        def scatter(i, total):
            for parity in range(2):
                hot = jnp.where(pick_scr[i, pl.ds(parity, 1)] == base, 1.0, 0.0).astype(BF16)
                total = total + dot_nt(hot, zeta_scr[i, parity].astype(BF16))
            return total

        spread = lax.fori_loop(0, rows, scatter, jnp.zeros((vocab, 2 * TAPS), F32))
        spread = spread[:, :TAPS] + spread[:, TAPS:]
        table = table_ref[...].astype(F32)
        scorer = scorer_ref[...].astype(F32)
        weight = weight_ref[...].astype(F32)
        grad, score_grad, conv = 0.0, 0.0, []
        for k in range(TAPS):
            one = spread[:, k : k + 1]
            total = sum_scr[pl.ds(k * vocab, vocab)] + one * scorer
            grad = grad + weight[k : k + 1] * total
            conv.append(jnp.sum(table * total, axis=0, keepdims=True))
            score_grad = score_grad + weight[k : k + 1] * jnp.sum(table * one, axis=0, keepdims=True)
        table_grad_ref[...] = grad
        rest_ref[...] = jnp.concatenate(conv + [score_grad, jnp.zeros((8 - TAPS - 1, width), F32)], axis=0)


def main(codes, table, conv_weight, scorer, scores, cotangent):
    rows, pairs, width = cotangent.shape
    vocab = table.shape[0]
    assert rows * 8 <= LANES
    padded = -(-pairs // LANES) * LANES + LANES
    tiles = width // LANES
    whole = lambda shape: pl.BlockSpec(shape, lambda i: (0,) * len(shape))
    return pl.pallas_call(
        main_kernel,
        grid=(rows,),
        in_specs=[
            whole(codes.shape),
            whole((vocab, width)),
            whole((TAPS, width)),
            whole((1, width)),
            whole((TAPS, vocab)),
            pl.BlockSpec((1, pairs, width), lambda i: (i, 0, 0)),
        ],
        out_specs=[
            pl.BlockSpec((1, pairs, width), lambda i: (i, 0, 0)),
            whole((vocab, width)),
            whole((8, width)),
        ],
        out_shape=[
            jax.ShapeDtypeStruct((rows, pairs, width), BF16),
            jax.ShapeDtypeStruct((vocab, width), F32),
            jax.ShapeDtypeStruct((8, width), F32),
        ],
        scratch_shapes=[
            pltpu.VMEM((rows, SPAN, padded), jnp.int32),
            pltpu.VMEM((rows, REACH * TAPS, padded), F32),
            pltpu.VMEM((rows, 16, padded), F32),
            pltpu.VMEM((rows, HALO + pairs, 16), F32),
            pltpu.VMEM((2 * TAPS, rows, padded), F32),
            pltpu.VMEM((2 * TAPS, rows, padded), F32),
            pltpu.VMEM((2, tiles, rows, HALO, LANES), F32),
            pltpu.VMEM((2 * tiles * (HALO + pairs), LANES), F32),
            pltpu.VMEM((2 * tiles * (HALO + pairs), LANES), F32),
            pltpu.VMEM((2 * tiles * (HALO + pairs), LANES), F32),
            pltpu.VMEM((pairs, LANES), F32),
            pltpu.VMEM((rows, 8, padded), F32),
            pltpu.VMEM((rows, 2, 2 * TAPS, padded), F32),
            pltpu.VMEM((TAPS, tiles, 8, LANES), F32),
            pltpu.VMEM((TAPS, 2, vocab, pairs), BF16),
            pltpu.VMEM((TAPS, 2, vocab, pairs), BF16),
            pltpu.VMEM((TAPS * vocab, width), F32),
        ],
        name="main",
    )(codes, table, conv_weight, scorer[None], scores, cotangent)


def reduce_all(table_grad, rest, rows_axis, seq_axis):
    ranks, parts = lax.axis_size(rows_axis), lax.axis_size(seq_axis)
    rank, part = lax.axis_index(rows_axis), lax.axis_index(seq_axis)

    def swap(x, axis, stride):
        return lax.ppermute(x, axis, [(i, i ^ stride) for i in range(lax.axis_size(axis))])

    vocab, width = table_grad.shape
    half = width // 2
    core = rank % 2
    whole = jnp.concatenate([table_grad, rest], axis=0)
    mine = lax.dynamic_slice_in_dim(whole, core * half, half, 1)
    other = lax.dynamic_slice_in_dim(whole, (1 - core) * half, half, 1)
    mine = mine + swap(other, rows_axis, 1)
    grad, rest = mine[:vocab], mine[vocab:]
    stride = parts // 2
    while stride:
        size = grad.shape[0] // 2
        bit = (part // stride) % 2
        sent = jnp.concatenate([lax.dynamic_slice_in_dim(grad, (1 - bit) * size, size, 0), rest], axis=0)
        kept = jnp.concatenate([lax.dynamic_slice_in_dim(grad, bit * size, size, 0), rest], axis=0)
        got = kept + swap(sent, seq_axis, stride)
        grad, rest = got[:size], got[size:]
        stride //= 2
    mine = jnp.concatenate([grad, rest], axis=0)
    stride = 2
    while stride < ranks:
        mine = mine + swap(mine, rows_axis, stride)
        stride *= 2
    other = swap(mine, rows_axis, 1)
    both = jnp.where(
        core == 0, jnp.concatenate([mine, other], axis=1), jnp.concatenate([other, mine], axis=1)
    )
    share = vocab // parts
    return both[:share], both[share : share + TAPS], both[share + TAPS]


def per_device(byte_ids, segment_ids, table, conv_weight, scorer, cotangent):
    parts = lax.axis_size("seq")
    codes = jnp.concatenate([byte_ids, segment_ids], axis=0)
    tail = codes[:, -LANES:]
    halo = lax.ppermute(tail, "seq", [(i, i + 1) for i in range(parts - 1)])
    halo = jnp.where(lax.axis_index("seq") == 0, -1, halo)
    scores = score_table(table, conv_weight, scorer)
    codes = jnp.concatenate([halo, codes], axis=1)
    blocks_out, table_grad, rest = main(codes, table, conv_weight, scorer, scores, cotangent)
    table_grad, conv_grad, scorer_grad = reduce_all(table_grad, rest, "rows", "seq")
    return (blocks_out, table_grad, conv_grad, scorer_grad)


def solution(mesh):
    return jax.shard_map(
        per_device,
        mesh=mesh,
        in_specs=(P("rows", "seq"), P("rows", "seq"), P(), P(), P(), P("rows", "seq", None)),
        out_specs=(P("rows", "seq", None), P("seq", None), P(), P()),
        check_vma=False,
    )
```

time: 95.3 us -> 76.8 us (0.81)
  Pallas kernels: 55.7 us -> 36.1 us
  waiting for transfers between devices: 17.8 us -> 19 us
    pallas_call x3 -> x2, Pallas kernels: 55.7 us -> 36.1 us  [the longest x1 34.2 us: main(): pl.pallas_call(main_kernel, grid=(rows,), in_specs=[whole(codes.shape), w...]
    ppermute x6, waiting for transfers between devices: 17.8 us -> 19 us  [swap(): lax.ppermute(x, axis, [(i, i ^ stride) for i in range(lax.axis_size(axis))])]
  transfers between devices with their start and end apart: 7 -> 7, of which waited for: 5 -> 6; matrix products, arithmetic and copies ran while one was open for 1% -> 2% of each run, Pallas kernels for 26% -> 3%
where the time goes in v2:
time: 76.8 us; the launch traced here: 76.3 us
  Pallas kernels  36.1 us (47%)
  waiting for transfers between devices  19 us (25%)
  starting transfers between devices  12.9 us (17%)
  local copies, waits for them, and re-layouts  6.67 us (9%)
  other arithmetic  0.82 us (1%)
  between operations  0.8 us (1%)
    pallas_call x1, Pallas kernels, main(): pl.pallas_call(main_kernel, grid=(rows,), in_specs=[whole(codes.shape), w...  34.2 us
    ppermute x6, waiting for transfers between devices, swap(): lax.ppermute(x, axis, [(i, i ^ stride) for i in range(lax.axis_size(axis))])  19 us
    ppermute x6, starting transfers between devices, swap(): lax.ppermute(x, axis, [(i, i ^ stride) for i in range(lax.axis_size(axis))])  8.08 us
    ppermute x1, starting transfers between devices, per_device(): halo = lax.ppermute(tail, 'seq', [(i, i + 1) for i in range(parts - 1)])  4.86 us
    pallas_call x1, Pallas kernels, score_table(): pl.pallas_call(score_kernel, out_shape=jax.ShapeDtypeStruct((TAPS, table....  1.92 us
    unnamed x2, local copies, waits for them, and re-layouts  1.91 us
    slice x3, local copies, waits for them, and re-layouts, reduce_all(): return (both[:share], both[share:share + TAPS], both[share + TAPS])  1.9 us
  transfers between devices with their start and end apart: 7, of which 6 were waited for; matrix products, arithmetic and copies ran while one was open for 2% of the time, Pallas kernels for 3%

profile of v2, /device:TPU:0, one launch (start us, length us, event | category | flops | bytes accessed | tf_op | source)
XLA Modules:
  0.0 76.3 jit_solution(6034845780241917866)
XLA Ops:
  0.6 0.7 constant_dynamic-update-slice_fusion.1
  1.4 0.7 constant_dynamic-update-slice_fusion
  2.1 4.9 %collective-permute-start = (s32[16,128]{1,0:T(8,128)S(1)}, s32[16,128]{1,0:T(8,128)S(1)}, u32[]{:S(2)}, u32[]{:S(2)}) collective-permute-start(s32[16,128]{1,0:T(8,128)S(1)} %slice.35), channel_id=1, source_target_pairs={{0,1},{1,2},{2,3},{4,5},{5,6},{6,7},{8,9},{9,10},{10,11},{12,13},{... | collective-permute-start | bytes 24584 | tf_op jit(solution)/shard_map/ppermute | solution.py:444
  7.0 1.3 %broadcast_in_dim.9.scorer_ref = bf16[1,768]{1,0:T(2,128)(2,1)} reshape(bf16[768]{0:T(1024)(128)(2,1)} %param.10) | data formatting | bytes 3072 | tf_op jit(solution)/shard_map/broadcast_in_dim | solution.py:400
  8.2 1.9 %score_table.1.score_ref = f32[4,256]{1,0:T(4,128)} custom-call(bf16[256,768]{1,0:T(8,128)(2,1)} %table_ref.3, bf16[4,768]{1,0:T(4,128)(2,1)} %weight_ref.3, bf16[1,768]{1,0:T(2,128)(2,1)} %broadcast_in_dim.9.scorer_ref), custom_call_target="tpu_custom_call" | custom-call | tf_op jit(solution)/shard_map/score_table/pallas_call | solution.py:43
  10.1 0.0 collective-permute-done
  10.2 0.6 pad_add_fusion.code_ref
  10.8 34.2 %main.1 = (bf16[8,256,768]{2,1,0:T(8,128)(2,1)}, f32[256,768]{1,0:T(8,128)}, f32[8,768]{1,0:T(8,128)}) custom-call(s32[16,640]{1,0:T(8,128)} %pad_add_fusion.code_ref, bf16[256,768]{1,0:T(8,128)(2,1)} %table_ref.3, bf16[4,768]{1,0:T(4,128)(2,1)} %weight_ref.3, bf16[1,768]{1,0:T(2,128)(2,1)} %broadcast_in_dim.9.scorer_ref, f32[4,256]{1,0:T(4,128)} %score_table.1.score_ref, ...), custom_call_target="tpu_custom_call" | custom-call | tf_op jit(solution)/shard_map/main/pallas_call | solution.py:359
  45.0 1.2 %constant_dynamic-update-slice_fusion.3 = f32[264,768]{1,0:T(8,128)S(1)} fusion(f32[256,768]{1,0:T(8,128)} %get-tuple-element.8), kind=kLoop, calls=%fused_computation.12 | loop fusion | bytes 1572864
  46.2 0.7 constant_dynamic-update-slice_fusion.2
  47.0 0.1 collective-permute-start.1
  47.1 1.7 %collective-permute-done.1 = f32[264,384]{1,0:T(8,128)S(1)} collective-permute-done((f32[264,384]{1,0:T(8,128)S(1)}, f32[264,384]{1,0:T(8,128)S(1)}, u32[]{:S(2)}, u32[]{:S(2)}) %collective-permute-start.1) | collective-permute-done | bytes 405536 | tf_op jit(solution)/shard_map/ppermute | solution.py:408
  48.8 0.1 dynamic-slice_add_fusion
  48.9 1.6 %collective-permute-start.2 = (f32[136,384]{1,0:T(8,128)S(1)}, f32[136,384]{1,0:T(8,128)S(1)}, u32[]{:S(2)}, u32[]{:S(2)}) collective-permute-start(f32[136,384]{1,0:T(8,128)S(1)} %pad_maximum_fusion), channel_id=1, source_target_pairs={{0,2},{1,3},{2,0},{3,1},{4,6},{5,7},{6,4},{7,5},{8,10},{9,11},{10,... | collective-permute-start | bytes 626696 | tf_op jit(solution)/shard_map/ppermute | solution.py:408
  50.5 5.7 %collective-permute-done.2 = f32[136,384]{1,0:T(8,128)S(1)} collective-permute-done((f32[136,384]{1,0:T(8,128)S(1)}, f32[136,384]{1,0:T(8,128)S(1)}, u32[]{:S(2)}, u32[]{:S(2)}) %collective-permute-start.2) | collective-permute-done | bytes 208928 | tf_op jit(solution)/shard_map/ppermute | solution.py:408
  56.3 1.6 %collective-permute-start.3 = (f32[72,384]{1,0:T(8,128)S(1)}, f32[72,384]{1,0:T(8,128)S(1)}, u32[]{:S(2)}, u32[]{:S(2)}) collective-permute-start(f32[72,384]{1,0:T(8,128)S(1)} %pad_maximum_fusion.2), channel_id=1, source_target_pairs={{0,1},{1,0},{2,3},{3,2},{4,5},{5,4},{6,7},{7,6},{8,9},{9,8},{10,11... | collective-permute-start | bytes 331784 | tf_op jit(solution)/shard_map/ppermute | solution.py:408
  57.9 3.2 %collective-permute-done.3 = f32[72,384]{1,0:T(8,128)S(1)} collective-permute-done((f32[72,384]{1,0:T(8,128)S(1)}, f32[72,384]{1,0:T(8,128)S(1)}, u32[]{:S(2)}, u32[]{:S(2)}) %collective-permute-start.3) | collective-permute-done | bytes 110624 | tf_op jit(solution)/shard_map/ppermute | solution.py:408
  61.2 1.6 %collective-permute-start.4 = (f32[72,384]{1,0:T(8,128)S(1)}, f32[72,384]{1,0:T(8,128)S(1)}, u32[]{:S(2)}, u32[]{:S(2)}) collective-permute-start(f32[72,384]{1,0:T(8,128)S(1)} %fusion.1), channel_id=1, source_target_pairs={{0,8},{4,12},{8,0},{12,4},{16,24},{20,28},{24,16},{28,20},{1,9},{5... | collective-permute-start | bytes 331784 | tf_op jit(solution)/shard_map/ppermute | solution.py:408
  62.8 3.2 %collective-permute-done.4 = f32[72,384]{1,0:T(8,128)S(1)} collective-permute-done((f32[72,384]{1,0:T(8,128)S(1)}, f32[72,384]{1,0:T(8,128)S(1)}, u32[]{:S(2)}, u32[]{:S(2)}) %collective-permute-start.4) | collective-permute-done | bytes 110624 | tf_op jit(solution)/shard_map/ppermute | solution.py:408
  66.0 3.1 %collective-permute-start.5 = (f32[72,384]{1,0:T(8,128)S(1)}, f32[72,384]{1,0:T(8,128)S(1)}, u32[]{:S(2)}, u32[]{:S(2)}) collective-permute-start(f32[72,384]{1,0:T(8,128)S(1)} %add.57), channel_id=1, source_target_pairs={{0,16},{4,20},{8,24},{12,28},{16,0},{20,4},{24,8},{28,12},{1,17},{... | collective-permute-start | bytes 331784 | tf_op jit(solution)/shard_map/ppermute | solution.py:408
  69.1 3.9 %collective-permute-done.5 = f32[72,384]{1,0:T(8,128)S(1)} collective-permute-done((f32[72,384]{1,0:T(8,128)S(1)}, f32[72,384]{1,0:T(8,128)S(1)}, u32[]{:S(2)}, u32[]{:S(2)}) %collective-permute-start.5) | collective-permute-done | bytes 110624 | tf_op jit(solution)/shard_map/ppermute | solution.py:408
  73.0 0.1 collective-permute-start.6
  73.1 1.3 %collective-permute-done.6 = f32[72,384]{1,0:T(8,128)S(1)} collective-permute-done((f32[72,384]{1,0:T(8,128)S(1)}, f32[72,384]{1,0:T(8,128)S(1)}, u32[]{:S(2)}, u32[]{:S(2)}) %collective-permute-start.6) | collective-permute-done | bytes 110624 | tf_op jit(solution)/shard_map/ppermute | solution.py:408
  74.5 0.7 slice.40
  75.1 0.6 slice.41
  75.7 0.6 slice_reduce_fusion
  (16 shorter events, 0.3 us)
Async XLA Ops:
  2.1 8.1 %collective-permute-start = (s32[16,128]{1,0:T(8,128)S(1)}, s32[16,128]{1,0:T(8,128)S(1)}, u32[]{:S(2)}, u32[]{:S(2)}) collective-permute-start(s32[16,128]{1,0:T(8,128)S(1)} %slice.35), channel_id=1, source_target_pairs={{0,1},{1,2},{2,3},{4,5},{5,6},{6,7},{8,9},{9,10},{10,11},{12,13},{... | collective-permute-start | bytes 24584 | tf_op jit(solution)/shard_map/ppermute | solution.py:444
  47.0 1.8 %collective-permute-start.1 = (f32[264,384]{1,0:T(8,128)S(1)}, f32[264,384]{1,0:T(8,128)S(1)}, u32[]{:S(2)}, u32[]{:S(2)}) collective-permute-start(f32[264,384]{1,0:T(8,128)S(1)} %constant_dynamic-slice_fusion.4), channel_id=1, source_target_pairs={{0,4},{4,0},{8,12},{12,8},{16,20},{20,16},{24,28},{28,24},{1,5},{5... | collective-permute-start | bytes 1216520 | tf_op jit(solution)/shard_map/ppermute | solution.py:408
  48.9 7.3 %collective-permute-start.2 = (f32[136,384]{1,0:T(8,128)S(1)}, f32[136,384]{1,0:T(8,128)S(1)}, u32[]{:S(2)}, u32[]{:S(2)}) collective-permute-start(f32[136,384]{1,0:T(8,128)S(1)} %pad_maximum_fusion), channel_id=1, source_target_pairs={{0,2},{1,3},{2,0},{3,1},{4,6},{5,7},{6,4},{7,5},{8,10},{9,11},{10,... | collective-permute-start | bytes 626696 | tf_op jit(solution)/shard_map/ppermute | solution.py:408
  56.3 4.8 %collective-permute-start.3 = (f32[72,384]{1,0:T(8,128)S(1)}, f32[72,384]{1,0:T(8,128)S(1)}, u32[]{:S(2)}, u32[]{:S(2)}) collective-permute-start(f32[72,384]{1,0:T(8,128)S(1)} %pad_maximum_fusion.2), channel_id=1, source_target_pairs={{0,1},{1,0},{2,3},{3,2},{4,5},{5,4},{6,7},{7,6},{8,9},{9,8},{10,11... | collective-permute-start | bytes 331784 | tf_op jit(solution)/shard_map/ppermute | solution.py:408
  61.2 4.8 %collective-permute-start.4 = (f32[72,384]{1,0:T(8,128)S(1)}, f32[72,384]{1,0:T(8,128)S(1)}, u32[]{:S(2)}, u32[]{:S(2)}) collective-permute-start(f32[72,384]{1,0:T(8,128)S(1)} %fusion.1), channel_id=1, source_target_pairs={{0,8},{4,12},{8,0},{12,4},{16,24},{20,28},{24,16},{28,20},{1,9},{5... | collective-permute-start | bytes 331784 | tf_op jit(solution)/shard_map/ppermute | solution.py:408
  66.0 7.0 %collective-permute-start.5 = (f32[72,384]{1,0:T(8,128)S(1)}, f32[72,384]{1,0:T(8,128)S(1)}, u32[]{:S(2)}, u32[]{:S(2)}) collective-permute-start(f32[72,384]{1,0:T(8,128)S(1)} %add.57), channel_id=1, source_target_pairs={{0,16},{4,20},{8,24},{12,28},{16,0},{20,4},{24,8},{28,12},{1,17},{... | collective-permute-start | bytes 331784 | tf_op jit(solution)/shard_map/ppermute | solution.py:408
  73.0 1.4 %collective-permute-start.6 = (f32[72,384]{1,0:T(8,128)S(1)}, f32[72,384]{1,0:T(8,128)S(1)}, u32[]{:S(2)}, u32[]{:S(2)}) collective-permute-start(f32[72,384]{1,0:T(8,128)S(1)} %add.58), channel_id=1, source_target_pairs={{0,4},{4,0},{8,12},{12,8},{16,20},{20,16},{24,28},{28,24},{1,5},{5... | collective-permute-start | bytes 331784 | tf_op jit(solution)/shard_map/ppermute | solution.py:408

commit v3 on v2

--- a/solution.py
+++ b/solution.py
@@ -6,6 +6,7 @@
 from jax.experimental import pallas as pl
 from jax.experimental.pallas import tpu as pltpu
 from jax.sharding import PartitionSpec as P
+
 
 TAPS = 4
 REACH = 5
@@ -35,7 +36,7 @@
 
 
 def score_kernel(table_ref, weight_ref, scorer_ref, score_ref):
-    hi, lo = split(weight_ref[...].astype(F32) * scorer_ref[...].astype(F32))
+    hi, lo = split(weight_ref[...].astype(F32) * scorer_ref[...].reshape(1, -1).astype(F32))
     score_ref[...] = dot_nt(hi, table_ref[...]) + dot_nt(lo, table_ref[...])
 
 
@@ -44,7 +45,7 @@
         score_kernel,
         out_shape=jax.ShapeDtypeStruct((TAPS, table.shape[0]), F32),
         name="score_table",
-    )(table, conv_weight, scorer[None])
+    )(table, conv_weight, scorer)
 
 
 def look_up(rows_of, index):
@@ -60,13 +61,13 @@
 
 
 HALO = 16
-GROUPS = 4
+GROUPS = 1
 
 
 def main_kernel(
-    code_ref, table_ref, weight_ref, scorer_ref, score_ref, cot_ref,
-    out_ref, table_grad_ref, rest_ref,
-    pick_scr, gam_scr, col_scr, column_scr, keep_scr, prob_scr, rim_scr, emb_a, emb_b, conv_scr, dcol_scr, prod_scr, zeta_scr,
+    core_ref, byte_ref, seg_ref, halo_ref, table_ref, weight_ref, scorer_ref, score_ref, cot_ref,
+    conv_ref, col_ref, mine_ref, other_ref,
+    pick_scr, gam_scr, col_scr, column_scr, keep_scr, prob_scr, rim_scr, emb_a, emb_b, mask_a, mask_b, dcol_scr, prod_scr, zeta_scr,
     weight_scr, mix_a, mix_b, sum_scr,
 ):
     rows, _, padded = pick_scr.shape
@@ -97,7 +98,15 @@
 
     @pl.when(row == 0)
     def _():
-        codes = code_ref[...].astype(F32).astype(BF16)
+        halo = halo_ref[...]
+        codes = jnp.concatenate(
+            [
+                jnp.concatenate([halo & (vocab - 1), byte_ref[...]], axis=1),
+                jnp.concatenate([halo >> (vocab.bit_length() - 1), seg_ref[...]], axis=1),
+            ],
+            axis=0,
+        )
+        codes = codes.astype(F32).astype(BF16)
         reach = codes.shape[1]
         ahead = reach - 2 * pairs
         at = lax.broadcasted_iota(jnp.int32, (reach, padded), 0) - ahead
@@ -151,7 +160,7 @@
     group = pairs // GROUPS
     part_v = vocab // GROUPS
 
-    embs, mixes = (emb_a, emb_b), (mix_a, mix_b)
+    embs, masks, mixes = (emb_a, emb_b), (mask_a, mask_b), (mix_a, mix_b)
 
     def spot(parity, d):
         return (parity * tiles + d) * deep
@@ -188,7 +197,7 @@
                     mixes[slot][k, 0, at, lane] = hi
                     mixes[slot][k, 1, at, lane] = lo
 
-    def gather(slot, j):
+    def gather(slot, j, first):
         cot = cot_ref[0]
         at = pl.ds(pl.multiple_of(j * part_v, 16), part_v)
         hi = jnp.concatenate([mixes[slot][k, 0, at] for k in range(TAPS)], axis=0)
@@ -198,49 +207,51 @@
         else:
             part = dot(hi, cot) + dot(lo, cot)
         for k in range(TAPS):
-            sum_scr[pl.ds(pl.multiple_of(k * vocab + j * part_v, 8), part_v)] += part[k * part_v : (k + 1) * part_v]
-
-    def conved(slot, at, column, d):
-        taken = [embs[slot][pl.ds(spot(s % 2, d) + at - s // 2, 8)] for s in range(REACH)]
-        for p in range(2):
-            total = weight_scr[0, d] * taken[p]
-            for k in range(1, TAPS):
-                keep = column[:, 2 + p * (TAPS - 1) + k - 1 :][:, :1]
-                total = total + keep * (weight_scr[k, d] * taken[p + k])
-            conv_scr[pl.ds(pl.multiple_of(spot(p, d) + at, 8), 8)] = total
+            to = pl.ds(pl.multiple_of(k * vocab + j * part_v, 8), part_v)
+            more = part[k * part_v : (k + 1) * part_v]
+            sum_scr[to] = more if first else sum_scr[to] + more
+
+    def spread(i, slot, at, to, size):
+        for t in range(0, size, 8):
+            column = column_scr[i, pl.ds(pl.multiple_of(at + t, 8), 8)]
+            for q in range(2 * (TAPS - 1)):
+                place = pl.multiple_of(q * (8 + pairs) + to + t, 8)
+                masks[slot][pl.ds(place, 8)] = jnp.broadcast_to(column[:, 2 + q : 3 + q], (8, LANES))
+
+    def conved(slot, at):
+        keep = [
+            masks[slot][pl.ds(pl.multiple_of(q * (8 + pairs) + at - HALO + 8, 8), 8)] for q in range(2 * (TAPS - 1))
+        ]
+        for d in range(tiles):
+            taken = [embs[slot][pl.ds(spot(s % 2, d) + at - s // 2, 8)] for s in range(REACH)]
+            for p in range(2):
+                total = weight_scr[0, d] * taken[p]
+                for k in range(1, TAPS):
+                    total = total + keep[p * (TAPS - 1) + k - 1] * (weight_scr[k, d] * taken[p + k])
+                conv_ref[pl.ds(pl.multiple_of(spot(p, d) + at, 8), 8)] = total
 
     lane_at = lax.broadcasted_iota(jnp.int32, (8, LANES), 1) - 8 * row
 
     def convolve(slot, j):
         for t in range(0, group, 8):
-            at = pl.multiple_of(HALO + j * group + t, 8)
-            column = column_scr[row, pl.ds(at, 8)]
-            for d in range(tiles):
-                conved(slot, at, column, d)
-
-    def blocks(j):
+            conved(slot, pl.multiple_of(HALO + j * group + t, 8))
+
+    def products(j):
         for t in range(0, group, 16):
             start = pl.multiple_of(j * group + t, 16)
-            column = [column_scr[row, pl.ds(pl.multiple_of(HALO + start + u, 8), 8)] for u in (0, 8)]
-            products = [[0.0] * REACH for _ in range(2)]
+            total = [[0.0] * REACH for _ in range(2)]
             for d in range(tiles):
-                lanes = pl.ds(d * LANES, LANES)
-                grad = cot_ref[0, pl.ds(start, 16), lanes].astype(F32)
-                out = []
+                grad = cot_ref[0, pl.ds(start, 16), pl.ds(d * LANES, LANES)].astype(F32)
                 for u in range(2):
                     at = HALO + start + 8 * u
-                    mixed = 0.0
                     for r in range(REACH):
-                        conv = conv_scr[pl.ds(spot(r % 2, d) + at - r // 2, 8)]
-                        products[u][r] = products[u][r] + grad[8 * u : 8 * u + 8] * conv
-                        mixed = mixed + column[u][:, 2 * TAPS + r : 2 * TAPS + r + 1] * conv
-                    out.append(mixed)
-                out_ref[0, pl.ds(start, 16), lanes] = jnp.concatenate(out, axis=0).astype(BF16)
+                        conv = conv_ref[pl.ds(spot(r % 2, d) + at - r // 2, 8)]
+                        total[u][r] = total[u][r] + grad[8 * u : 8 * u + 8] * conv
             for u in range(2):
                 to = pl.ds(pl.multiple_of(start + 8 * u, 8), 8)
                 found = dcol_scr[to]
                 for r in range(REACH):
-                    found = jnp.where(lane_at == r, jnp.sum(products[u][r], axis=1, keepdims=True), found)
+                    found = jnp.where(lane_at == r, jnp.sum(total[u][r], axis=1, keepdims=True), found)
                 dcol_scr[to] = found
 
     @pl.when(row == 0)
@@ -263,35 +274,38 @@
             for d in range(tiles):
                 lanes = pl.ds(d * LANES, LANES)
                 weight_scr[k, d] = jnp.broadcast_to(weight_ref[k : k + 1, lanes].astype(F32), (8, LANES))
-        sum_scr[...] = jnp.zeros_like(sum_scr)
         dcol_scr[...] = jnp.zeros_like(dcol_scr)
         embed_rim(0, 0)
+        spread(0, 0, HALO - 8, 0, 8)
+        col_ref[...] = col_scr[...]
 
         @pl.loop(0, GROUPS)
         def _(j):
+            spread(0, 0, HALO + j * group, 8 + j * group, group)
             embed(0, 0, j)
             mixing(0, 0, j)
 
-    def work(slot, more):
+    def work(slot, more, first=False):
         if more:
             embed_rim(row + 1, 1 - slot)
-        rim = column_scr[row, pl.ds(HALO - 8, 8)]
-        for d in range(tiles):
-            conved(slot, HALO - 8, rim, d)
+            spread(row + 1, 1 - slot, HALO - 8, 0, 8)
+        conved(slot, HALO - 8)
 
         @pl.loop(0, GROUPS)
         def _(j):
             convolve(slot, j)
-            gather(slot, j)
+            gather(slot, j, first)
             if more:
+                spread(row + 1, 1 - slot, HALO + j * group, 8 + j * group, group)
                 mixing(row + 1, 1 - slot, j)
                 embed(row + 1, 1 - slot, j)
-            blocks(j)
+            products(j)
 
     last = rows - 1
-    pl.when((row < last) & (row % 2 == 0))(lambda: work(0, True))
+    pl.when(row == 0)(lambda: work(0, last > 0, True))
+    pl.when((row > 0) & (row < last) & (row % 2 == 0))(lambda: work(0, True))
     pl.when((row < last) & (row % 2 == 1))(lambda: work(1, True))
-    pl.when(row == last)(lambda: work(last % 2, False))
+    pl.when((row > 0) & (row == last))(lambda: work(last % 2, False))
 
     @pl.when(row == rows - 1)
     def _():
@@ -327,29 +341,87 @@
                     zeta_scr[i, parity, TAPS + k : TAPS + k + 1] = low[i : i + 1]
         base = lax.broadcasted_iota(jnp.int32, (vocab, padded), 0)
 
-        def scatter(i, total):
-            for parity in range(2):
-                hot = jnp.where(pick_scr[i, pl.ds(parity, 1)] == base, 1.0, 0.0).astype(BF16)
-                total = total + dot_nt(hot, zeta_scr[i, parity].astype(BF16))
-            return total
-
-        spread = lax.fori_loop(0, rows, scatter, jnp.zeros((vocab, 2 * TAPS), F32))
-        spread = spread[:, :TAPS] + spread[:, TAPS:]
+        found = jnp.zeros((vocab, 2 * TAPS), F32)
+        for i in range(rows):
+            hot = [jnp.where(pick_scr[i, pl.ds(p, 1)] == base, 1.0, 0.0).astype(BF16) for p in range(2)]
+            found = found + dot_nt(
+                jnp.concatenate(hot, axis=1),
+                jnp.concatenate([zeta_scr[i, p].astype(BF16) for p in range(2)], axis=1),
+            )
+        found = found[:, :TAPS] + found[:, TAPS:]
+        scorer = scorer_ref[...].reshape(1, -1).astype(F32)
+        weight = weight_ref[...].astype(F32)
         table = table_ref[...].astype(F32)
-        scorer = scorer_ref[...].astype(F32)
-        weight = weight_ref[...].astype(F32)
-        grad, score_grad, conv = 0.0, 0.0, []
+        hi, lo = split(found)
+        tall = lambda a, b: lax.dot_general(a, b, (((0,), (0,)), ((), ())), preferred_element_type=F32)
+        sums = tall(hi, table_ref[...]) + tall(lo, table_ref[...])
+        near, rest = split(weight * scorer)
+        grad = dot(
+            jnp.concatenate([hi, lo, hi], axis=1), jnp.concatenate([near, near, rest], axis=0)
+        )
+        conv, score_grad = [], 0.0
         for k in range(TAPS):
-            one = spread[:, k : k + 1]
-            total = sum_scr[pl.ds(k * vocab, vocab)] + one * scorer
+            total = sum_scr[pl.ds(k * vocab, vocab)]
             grad = grad + weight[k : k + 1] * total
-            conv.append(jnp.sum(table * total, axis=0, keepdims=True))
-            score_grad = score_grad + weight[k : k + 1] * jnp.sum(table * one, axis=0, keepdims=True)
-        table_grad_ref[...] = grad
-        rest_ref[...] = jnp.concatenate(conv + [score_grad, jnp.zeros((8 - TAPS - 1, width), F32)], axis=0)
-
-
-def main(codes, table, conv_weight, scorer, scores, cotangent):
+            conv.append(jnp.sum(table * total, axis=0, keepdims=True) + scorer * sums[k : k + 1])
+            score_grad = score_grad + weight[k : k + 1] * sums[k : k + 1]
+        rest = jnp.concatenate(conv + [score_grad, jnp.zeros((8 - TAPS - 1, width), F32)], axis=0)
+        half = width // 2
+        first = core_ref[0] == 0
+        for at, value in ((0, grad), (vocab, rest)):
+            to = pl.ds(at, value.shape[0])
+            left, right = value[:, :half], value[:, half:]
+            mine_ref[to] = jnp.where(first, left, right)
+            other_ref[to] = jnp.where(first, right, left)
+
+
+def blocks_kernel(*refs):
+    conv_refs, col_ref, out_ref = refs[: 2 * STREAMS], refs[2 * STREAMS], refs[-1]
+    pairs, width = out_ref.shape[1:]
+    column = jnp.transpose(col_ref[0])
+    each = width // LANES // STREAMS
+    for t in range(0, pairs, 16):
+        share = [
+            [jnp.broadcast_to(column[t + u : t + u + 8, q : q + 1], (8, LANES)) for q in range(2 * TAPS, 2 * TAPS + REACH)]
+            for u in (0, 8)
+        ]
+        for d in range(width // LANES):
+            out = []
+            for u in range(2):
+                total = 0.0
+                for r in range(REACH):
+                    at = d % each * (HALO + pairs) + HALO + t + 8 * u - r // 2
+                    total = total + share[u][r] * conv_refs[r % 2 * STREAMS + d // each][0, 0, pl.ds(at, 8)]
+                out.append(total)
+            out_ref[0, pl.ds(t, 16), pl.ds(d * LANES, LANES)] = jnp.concatenate(out, axis=0).astype(BF16)
+
+
+STREAMS = 3
+
+
+def blocks(conv, columns, pairs, width, start, stop, before=None):
+    rows = conv.shape[0]
+    conv = conv.reshape(rows, 2 * STREAMS, -1, LANES)
+    part = lambda n: pl.BlockSpec((1, 1) + conv.shape[2:], lambda i: (i + start, n, 0, 0))
+    return pl.pallas_call(
+        blocks_kernel,
+        grid=(stop - start,),
+        in_specs=[part(n) for n in range(2 * STREAMS)]
+        + [pl.BlockSpec((1,) + columns.shape[1:], lambda i: (i + start, 0, 0))]
+        + ([] if before is None else [pl.BlockSpec(memory_space=pl.ANY)]),
+        out_specs=pl.BlockSpec((1, pairs, width), lambda i: (i + start, 0, 0)),
+        out_shape=jax.ShapeDtypeStruct((rows, pairs, width), BF16),
+        input_output_aliases={} if before is None else {2 * STREAMS + 1: 0},
+        cost_estimate=pl.CostEstimate(
+            flops=9 * (stop - start) * pairs * width,
+            bytes_accessed=(stop - start) * (4 * conv.size // rows + 2 * pairs * width),
+            transcendentals=0,
+        ),
+        name="blocks",
+    )(*[conv] * (2 * STREAMS), columns, *([] if before is None else [before]))
+
+
+def main(core, byte_ids, segment_ids, halo, table, conv_weight, scorer, scores, cotangent):
     rows, pairs, width = cotangent.shape
     vocab = table.shape[0]
     assert rows * 8 <= LANES
@@ -360,22 +432,27 @@
         main_kernel,
         grid=(rows,),
         in_specs=[
-            whole(codes.shape),
+            pl.BlockSpec(memory_space=pltpu.SMEM),
+            whole(byte_ids.shape),
+            whole(segment_ids.shape),
+            whole(halo.shape),
             whole((vocab, width)),
             whole((TAPS, width)),
-            whole((1, width)),
+            whole((width,)),
             whole((TAPS, vocab)),
             pl.BlockSpec((1, pairs, width), lambda i: (i, 0, 0)),
         ],
         out_specs=[
-            pl.BlockSpec((1, pairs, width), lambda i: (i, 0, 0)),
-            whole((vocab, width)),
-            whole((8, width)),
+            pl.BlockSpec((None, 2 * tiles * (HALO + pairs), LANES), lambda i: (i, 0, 0)),
+            whole((rows, 16, padded)),
+            whole((vocab + 8, width // 2)),
+            whole((vocab + 8, width // 2)),
         ],
         out_shape=[
-            jax.ShapeDtypeStruct((rows, pairs, width), BF16),
-            jax.ShapeDtypeStruct((vocab, width), F32),
-            jax.ShapeDtypeStruct((8, width), F32),
+            jax.ShapeDtypeStruct((rows, 2 * tiles * (HALO + pairs), LANES), F32),
+            jax.ShapeDtypeStruct((rows, 16, padded), F32),
+            jax.ShapeDtypeStruct((vocab + 8, width // 2), F32),
+            jax.ShapeDtypeStruct((vocab + 8, width // 2), F32),
         ],
         scratch_shapes=[
             pltpu.VMEM((rows, SPAN, padded), jnp.int32),
@@ -387,7 +464,8 @@
             pltpu.VMEM((2, tiles, rows, HALO, LANES), F32),
             pltpu.VMEM((2 * tiles * (HALO + pairs), LANES), F32),
             pltpu.VMEM((2 * tiles * (HALO + pairs), LANES), F32),
-            pltpu.VMEM((2 * tiles * (HALO + pairs), LANES), F32),
+            pltpu.VMEM((2 * (TAPS - 1) * (8 + pairs), LANES), F32),
+            pltpu.VMEM((2 * (TAPS - 1) * (8 + pairs), LANES), F32),
             pltpu.VMEM((pairs, LANES), F32),
             pltpu.VMEM((rows, 8, padded), F32),
             pltpu.VMEM((rows, 2, 2 * TAPS, padded), F32),
@@ -397,57 +475,52 @@
             pltpu.VMEM((TAPS * vocab, width), F32),
         ],
         name="main",
-    )(codes, table, conv_weight, scorer[None], scores, cotangent)
-
-
-def reduce_all(table_grad, rest, rows_axis, seq_axis):
+    )(core, byte_ids, segment_ids, halo, table, conv_weight, scorer, scores, cotangent)
+
+
+def add_parts(mine, other, rows_axis, seq_axis, vocab):
     ranks, parts = lax.axis_size(rows_axis), lax.axis_size(seq_axis)
     rank, part = lax.axis_index(rows_axis), lax.axis_index(seq_axis)
-
-    def swap(x, axis, stride):
-        return lax.ppermute(x, axis, [(i, i ^ stride) for i in range(lax.axis_size(axis))])
-
-    vocab, width = table_grad.shape
-    half = width // 2
-    core = rank % 2
-    whole = jnp.concatenate([table_grad, rest], axis=0)
-    mine = lax.dynamic_slice_in_dim(whole, core * half, half, 1)
-    other = lax.dynamic_slice_in_dim(whole, (1 - core) * half, half, 1)
-    mine = mine + swap(other, rows_axis, 1)
-    grad, rest = mine[:vocab], mine[vocab:]
-    stride = parts // 2
-    while stride:
-        size = grad.shape[0] // 2
-        bit = (part // stride) % 2
-        sent = jnp.concatenate([lax.dynamic_slice_in_dim(grad, (1 - bit) * size, size, 0), rest], axis=0)
-        kept = jnp.concatenate([lax.dynamic_slice_in_dim(grad, bit * size, size, 0), rest], axis=0)
-        got = kept + swap(sent, seq_axis, stride)
-        grad, rest = got[:size], got[size:]
-        stride //= 2
-    mine = jnp.concatenate([grad, rest], axis=0)
+    share = vocab // parts
+
+    def swap(x, stride):
+        return lax.ppermute(x, rows_axis, [(i, i ^ stride) for i in range(ranks)])
+
+    mine = mine + swap(other, 1)
+    rest = mine[vocab:]
+    piece = lambda n: jnp.concatenate(
+        [lax.dynamic_slice_in_dim(mine, (part + n) % parts * share, share, 0), rest], axis=0
+    )
+    total = piece(0)
+    for n in range(1, parts):
+        total = total + lax.ppermute(piece(n), seq_axis, [(i, (i + n) % parts) for i in range(parts)])
     stride = 2
     while stride < ranks:
-        mine = mine + swap(mine, rows_axis, stride)
+        total = total + swap(total, stride)
         stride *= 2
-    other = swap(mine, rows_axis, 1)
-    both = jnp.where(
-        core == 0, jnp.concatenate([mine, other], axis=1), jnp.concatenate([other, mine], axis=1)
+    other = swap(total, 1)
+    whole = jnp.where(
+        rank % 2 == 0, jnp.concatenate([total, other], axis=1), jnp.concatenate([other, total], axis=1)
     )
-    share = vocab // parts
-    return both[:share], both[share : share + TAPS], both[share + TAPS]
+    return whole[:share], whole[share : share + TAPS], whole[share + TAPS]
 
 
 def per_device(byte_ids, segment_ids, table, conv_weight, scorer, cotangent):
     parts = lax.axis_size("seq")
-    codes = jnp.concatenate([byte_ids, segment_ids], axis=0)
-    tail = codes[:, -LANES:]
+    vocab = table.shape[0]
+    rows, pairs, width = cotangent.shape
+    tail = byte_ids[:, -LANES:] + vocab * segment_ids[:, -LANES:]
     halo = lax.ppermute(tail, "seq", [(i, i + 1) for i in range(parts - 1)])
-    halo = jnp.where(lax.axis_index("seq") == 0, -1, halo)
+    halo = jnp.where(lax.axis_index("seq") == 0, -vocab, halo)
+    core = (lax.axis_index("rows") % 2)[None]
     scores = score_table(table, conv_weight, scorer)
-    codes = jnp.concatenate([halo, codes], axis=1)
-    blocks_out, table_grad, rest = main(codes, table, conv_weight, scorer, scores, cotangent)
-    table_grad, conv_grad, scorer_grad = reduce_all(table_grad, rest, "rows", "seq")
-    return (blocks_out, table_grad, conv_grad, scorer_grad)
+    conv, columns, mine, other = main(core, byte_ids, segment_ids, halo, table, conv_weight, scorer, scores, cotangent)
+    cuts = (0, rows // 2, rows - rows // 4, rows)
+    out = None
+    for n in range(3):
+        out = blocks(conv, columns, pairs, width, cuts[n], cuts[n + 1], out)
+    table_grad, conv_grad, scorer_grad = add_parts(mine, other, "rows", "seq", vocab)
+    return (out, table_grad, conv_grad, scorer_grad)
 
 
 def solution(mesh):

time: 76.8 us -> 74 us (0.964)
  waiting for transfers between devices: 19 us -> 13.3 us
  local copies, waits for them, and re-layouts: 6.67 us -> 1.94 us
  Pallas kernels: 36.1 us -> 40.4 us
  starting transfers between devices: 12.9 us -> 14.8 us
  other arithmetic: 0.82 us -> 2.46 us
    ppermute x6 -> x7, waiting for transfers between devices: 19 us -> 13.3 us  [the longest x4 9.3 us: swap(): return lax.ppermute(x, rows_axis, [(i, i ^ stride) for i in range(ranks)])]
    pallas_call x1 -> x4, Pallas kernels: 34.2 us -> 38.4 us  [the longest x1 26.9 us: main(): pl.pallas_call(main_kernel, grid=(rows,), in_specs=[pl.BlockSpec(memory_s...]
    unnamed x2 -> x0, local copies, waits for them, and re-layouts: 1.91 us -> none
    ppermute x6 -> x7, starting transfers between devices: 8.08 us -> 9.92 us  [the longest x3 5.55 us: add_parts(): lax.ppermute(piece(n), seq_axis, [(i, (i + n) % parts) for i in range(par...]
    add x5, other arithmetic: 0.13 us -> 1.81 us  [the longest x1 1.04 us: add_parts(): mine = mine + swap(other, 1)]
    concatenate x2 -> x0, local copies, waits for them, and re-layouts: 1.46 us -> none  [the longest x1 0.74 us: reduce_all(): whole = jnp.concatenate([table_grad, rest], axis=0)]
    broadcast_in_dim x1 -> x0, local copies, waits for them, and re-layouts: 1.26 us -> none  [main(): scorer[None]]
    slice x8 -> x4, local copies, waits for them, and re-layouts: 1.95 us -> 1.9 us  [the longest x3 1.9 us: add_parts(): return (whole[:share], whole[share:share + TAPS], whole[share + TAPS])]
  transfers between devices with their start and end apart: 7 -> 8, of which waited for: 6 -> 6; matrix products, arithmetic and copies ran while one was open for 2% -> 0% of each run, Pallas kernels for 3% -> 18%
where the time goes in v3:
time: 74 us; the launch traced here: 73.7 us
  Pallas kernels  40.4 us (55%)
  starting transfers between devices  14.8 us (20%)
  waiting for transfers between devices  13.3 us (18%)
  other arithmetic  2.46 us (3%)
  local copies, waits for them, and re-layouts  1.94 us (3%)
  between operations  0.77 us (1%)
    pallas_call x1, Pallas kernels, main(): pl.pallas_call(main_kernel, grid=(rows,), in_specs=[pl.BlockSpec(memory_s...  26.9 us
    pallas_call x3, Pallas kernels, blocks(): pl.pallas_call(blocks_kernel, grid=(stop - start,), in_specs=[part(n) for...  11.6 us
    ppermute x4, waiting for transfers between devices, swap(): return lax.ppermute(x, rows_axis, [(i, i ^ stride) for i in range(ranks)])  9.3 us
    ppermute x3, starting transfers between devices, add_parts(): lax.ppermute(piece(n), seq_axis, [(i, (i + n) % parts) for i in range(par...  5.55 us
    ppermute x1, starting transfers between devices, per_device(): halo = lax.ppermute(tail, 'seq', [(i, i + 1) for i in range(parts - 1)])  4.86 us
    ppermute x4, starting transfers between devices, swap(): return lax.ppermute(x, rows_axis, [(i, i ^ stride) for i in range(ranks)])  4.38 us
    ppermute x3, waiting for transfers between devices, add_parts(): lax.ppermute(piece(n), seq_axis, [(i, (i + n) % parts) for i in range(par...  4.02 us
    pallas_call x1, Pallas kernels, score_table(): pl.pallas_call(score_kernel, out_shape=jax.ShapeDtypeStruct((TAPS, table....  1.93 us
  transfers between devices with their start and end apart: 8, of which 6 were waited for; matrix products, arithmetic and copies ran while one was open for 0% of the time, Pallas kernels for 18%

profile of v3, /device:TPU:0, one launch (start us, length us, event | category | flops | bytes accessed | tf_op | source)
XLA Modules:
  0.0 73.7 jit_solution(13591545372630138999)
XLA Ops:
  0.6 0.7 multiply_add_fusion
  1.3 4.9 %collective-permute-start = (s32[8,128]{1,0:T(8,128)S(1)}, s32[8,128]{1,0:T(8,128)S(1)}, u32[]{:S(2)}, u32[]{:S(2)}) collective-permute-start(s32[8,128]{1,0:T(8,128)S(1)} %multiply_add_fusion), channel_id=1, source_target_pairs={{0,1},{1,2},{2,3},{4,5},{5,6},{6,7},{8,9},{9,10},{10,11},{12,13},{... | collective-permute-start | bytes 12296 | tf_op jit(solution)/shard_map/ppermute | solution.py:513
  6.2 1.9 %score_table.1.score_ref = f32[4,256]{1,0:T(4,128)} custom-call(bf16[256,768]{1,0:T(8,128)(2,1)} %table_ref.3, bf16[4,768]{1,0:T(4,128)(2,1)} %weight_ref.3, bf16[768]{0:T(1024)(128)(2,1)} %scorer_ref.3), custom_call_target="tpu_custom_call" | custom-call | tf_op jit(solution)/shard_map/score_table/pallas_call | solution.py:44
  8.2 0.0 collective-permute-done
  8.2 0.6 broadcast_select_fusion.halo_ref
  8.8 26.9 %main.1 = (f32[8,3264,128]{2,1,0:T(8,128)}, f32[8,16,384]{2,1,0:T(8,128)}, f32[264,384]{1,0:T(8,128)}, f32[264,384]{1,0:T(8,128)}) custom-call(s32[1]{0:T(128)} %bitcast.core_ref, s32[8,512]{1,0:T(8,128)} %byte_ref.1, s32[8,512]{1,0:T(8,128)} %seg_ref.1, s32[8,128]{1,0:T(8,128)} %broadcast_select_fusion.halo_ref, bf16[256,768]{1,0:T(8,128)(2,1)} %table_ref.3, ...), custom_call_target="tpu_custom_call" | custom-call | tf_op jit(solution)/shard_map/main/pallas_call | solution.py:431
  35.6 0.0 collective-permute-start.1
  35.7 1.9 %collective-permute-done.1 = f32[264,384]{1,0:T(8,128)S(1)} collective-permute-done((f32[264,384]{1,0:T(8,128)}, f32[264,384]{1,0:T(8,128)S(1)}, u32[]{:S(2)}, u32[]{:S(2)}) %collective-permute-start.1) | collective-permute-done | bytes 405536 | tf_op jit(solution)/shard_map/ppermute | solution.py:487
  37.6 1.0 %add.61 = f32[264,384]{1,0:T(8,128)S(1)} add(f32[264,384]{1,0:T(8,128)} %get-tuple-element.10, f32[264,384]{1,0:T(8,128)S(1)} %collective-permute-done.1) | non-fusion elementwise | flops 101376 | bytes 1216512 | tf_op jit(solution)/shard_map/add | solution.py:489
  38.7 1.7 %collective-permute-start.2 = (f32[72,384]{1,0:T(8,128)S(1)}, f32[72,384]{1,0:T(8,128)S(1)}, u32[]{:S(2)}, u32[]{:S(2)}) collective-permute-start(f32[72,384]{1,0:T(8,128)S(1)} %get-tuple-element.16), channel_id=1, source_target_pairs={{0,1},{1,2},{2,3},{3,0},{4,5},{5,6},{6,7},{7,4},{8,9},{9,10},{10,1... | collective-permute-start | bytes 331784 | tf_op jit(solution)/shard_map/ppermute | solution.py:496
  40.4 1.5 %collective-permute-start.3 = (f32[72,384]{1,0:T(8,128)S(1)}, f32[72,384]{1,0:T(8,128)S(1)}, u32[]{:S(2)}, u32[]{:S(2)}) collective-permute-start(f32[72,384]{1,0:T(8,128)S(1)} %get-tuple-element.17), channel_id=1, source_target_pairs={{0,2},{1,3},{2,0},{3,1},{4,6},{5,7},{6,4},{7,5},{8,10},{9,11},{10,... | collective-permute-start | bytes 331784 | tf_op jit(solution)/shard_map/ppermute | solution.py:496
  41.9 2.3 %collective-permute-start.4 = (f32[72,384]{1,0:T(8,128)S(1)}, f32[72,384]{1,0:T(8,128)S(1)}, u32[]{:S(2)}, u32[]{:S(2)}) collective-permute-start(f32[72,384]{1,0:T(8,128)S(1)} %get-tuple-element.18), channel_id=1, source_target_pairs={{0,3},{1,0},{2,1},{3,2},{4,7},{5,4},{6,5},{7,6},{8,11},{9,8},{10,9... | collective-permute-start | bytes 331784 | tf_op jit(solution)/shard_map/ppermute | solution.py:496
  44.3 0.6 collective-permute-done.2
  44.9 2.2 %collective-permute-done.3 = f32[72,384]{1,0:T(8,128)S(1)} collective-permute-done((f32[72,384]{1,0:T(8,128)S(1)}, f32[72,384]{1,0:T(8,128)S(1)}, u32[]{:S(2)}, u32[]{:S(2)}) %collective-permute-start.3) | collective-permute-done | bytes 110624 | tf_op jit(solution)/shard_map/ppermute | solution.py:496
  47.1 1.2 %collective-permute-done.4 = f32[72,384]{1,0:T(8,128)S(1)} collective-permute-done((f32[72,384]{1,0:T(8,128)S(1)}, f32[72,384]{1,0:T(8,128)S(1)}, u32[]{:S(2)}, u32[]{:S(2)}) %collective-permute-start.4) | collective-permute-done | bytes 110624 | tf_op jit(solution)/shard_map/ppermute | solution.py:496
  48.3 1.6 %collective-permute-start.5 = (f32[72,384]{1,0:T(8,128)S(1)}, f32[72,384]{1,0:T(8,128)S(1)}, u32[]{:S(2)}, u32[]{:S(2)}) collective-permute-start(f32[72,384]{1,0:T(8,128)S(1)} %fusion.2), channel_id=1, source_target_pairs={{0,8},{4,12},{8,0},{12,4},{16,24},{20,28},{24,16},{28,20},{1,9},{5... | collective-permute-start | bytes 331784 | tf_op jit(solution)/shard_map/ppermute | solution.py:487
  50.0 3.2 %collective-permute-done.5 = f32[72,384]{1,0:T(8,128)S(1)} collective-permute-done((f32[72,384]{1,0:T(8,128)S(1)}, f32[72,384]{1,0:T(8,128)S(1)}, u32[]{:S(2)}, u32[]{:S(2)}) %collective-permute-start.5) | collective-permute-done | bytes 110624 | tf_op jit(solution)/shard_map/ppermute | solution.py:487
  53.2 2.7 %collective-permute-start.6 = (f32[72,384]{1,0:T(8,128)S(1)}, f32[72,384]{1,0:T(8,128)S(1)}, u32[]{:S(2)}, u32[]{:S(2)}) collective-permute-start(f32[72,384]{1,0:T(8,128)S(1)} %add.76), channel_id=1, source_target_pairs={{0,16},{4,20},{8,24},{12,28},{16,0},{20,4},{24,8},{28,12},{1,17},{... | collective-permute-start | bytes 331784 | tf_op jit(solution)/shard_map/ppermute | solution.py:487
  55.8 4.2 %collective-permute-done.6 = f32[72,384]{1,0:T(8,128)S(1)} collective-permute-done((f32[72,384]{1,0:T(8,128)S(1)}, f32[72,384]{1,0:T(8,128)S(1)}, u32[]{:S(2)}, u32[]{:S(2)}) %collective-permute-start.6) | collective-permute-done | bytes 110624 | tf_op jit(solution)/shard_map/ppermute | solution.py:487
  60.1 0.1 collective-permute-start.7
  60.2 5.3 %blocks.3.refs_7_ = bf16[8,256,768]{2,1,0:T(8,128)(2,1)} custom-call(f32[8,6,544,128]{3,2,1,0:T(8,128)} %bitcast.2, f32[8,6,544,128]{3,2,1,0:T(8,128)} %bitcast.3, f32[8,6,544,128]{3,2,1,0:T(8,128)} %bitcast.4, f32[8,6,544,128]{3,2,1,0:T(8,128)} %bitcast.5, f32[8,6,544,128]{3,2,1,0:T(8,128)} %bitcast.6, f32[8,6,544,128]{3,2,1,0:T(8,128)} %bitcast.7, ...), custom_call_target="tpu_custom_call" | custom-call | flops 7077888 | bytes 8257536 | tf_op jit(solution)/shard_map/blocks/pallas_call | solution.py:406
  65.5 3.1 %blocks.4.refs_7_ = bf16[8,256,768]{2,1,0:T(8,128)(2,1)} custom-call(f32[8,6,544,128]{3,2,1,0:T(8,128)} %bitcast.8, f32[8,6,544,128]{3,2,1,0:T(8,128)} %bitcast.9, f32[8,6,544,128]{3,2,1,0:T(8,128)} %bitcast.10, f32[8,6,544,128]{3,2,1,0:T(8,128)} %bitcast.11, f32[8,6,544,128]{3,2,1,0:T(8,128)} %bitcast.12, ...), custom_call_target="tpu_custom_call", output_to_operand_aliasing={{}: (7, {})} | custom-call | flops 3538944 | bytes 4128768 | tf_op jit(solution)/shard_map/blocks/pallas_call | solution.py:406
  68.6 3.1 %blocks.5 = bf16[8,256,768]{2,1,0:T(8,128)(2,1)} custom-call(f32[8,6,544,128]{3,2,1,0:T(8,128)} %bitcast.14, f32[8,6,544,128]{3,2,1,0:T(8,128)} %bitcast.15, f32[8,6,544,128]{3,2,1,0:T(8,128)} %bitcast.16, f32[8,6,544,128]{3,2,1,0:T(8,128)} %bitcast.17, f32[8,6,544,128]{3,2,1,0:T(8,128)} %bitcast.18, ...), custom_call_target="tpu_custom_call", output_to_operand_aliasing={{}: (7, {})} | custom-call | flops 3538944 | bytes 4128768 | tf_op jit(solution)/shard_map/blocks/pallas_call | solution.py:406
  71.7 0.0 collective-permute-done.7
  71.8 0.6 slice_reduce_fusion
  72.4 0.6 slice.26
  73.0 0.7 slice.25
  (7 shorter events, 0.2 us)
Async XLA Ops:
  1.3 6.8 %collective-permute-start = (s32[8,128]{1,0:T(8,128)S(1)}, s32[8,128]{1,0:T(8,128)S(1)}, u32[]{:S(2)}, u32[]{:S(2)}) collective-permute-start(s32[8,128]{1,0:T(8,128)S(1)} %multiply_add_fusion), channel_id=1, source_target_pairs={{0,1},{1,2},{2,3},{4,5},{5,6},{6,7},{8,9},{9,10},{10,11},{12,13},{... | collective-permute-start | bytes 12296 | tf_op jit(solution)/shard_map/ppermute | solution.py:513
  35.6 2.0 %collective-permute-start.1 = (f32[264,384]{1,0:T(8,128)}, f32[264,384]{1,0:T(8,128)S(1)}, u32[]{:S(2)}, u32[]{:S(2)}) collective-permute-start(f32[264,384]{1,0:T(8,128)} %get-tuple-element.11), channel_id=1, source_target_pairs={{0,4},{4,0},{8,12},{12,8},{16,20},{20,16},{24,28},{28,24},{1,5},{5... | collective-permute-start | bytes 1216520 | tf_op jit(solution)/shard_map/ppermute | solution.py:487
  38.7 6.2 %collective-permute-start.2 = (f32[72,384]{1,0:T(8,128)S(1)}, f32[72,384]{1,0:T(8,128)S(1)}, u32[]{:S(2)}, u32[]{:S(2)}) collective-permute-start(f32[72,384]{1,0:T(8,128)S(1)} %get-tuple-element.16), channel_id=1, source_target_pairs={{0,1},{1,2},{2,3},{3,0},{4,5},{5,6},{6,7},{7,4},{8,9},{9,10},{10,1... | collective-permute-start | bytes 331784 | tf_op jit(solution)/shard_map/ppermute | solution.py:496
  40.4 6.7 %collective-permute-start.3 = (f32[72,384]{1,0:T(8,128)S(1)}, f32[72,384]{1,0:T(8,128)S(1)}, u32[]{:S(2)}, u32[]{:S(2)}) collective-permute-start(f32[72,384]{1,0:T(8,128)S(1)} %get-tuple-element.17), channel_id=1, source_target_pairs={{0,2},{1,3},{2,0},{3,1},{4,6},{5,7},{6,4},{7,5},{8,10},{9,11},{10,... | collective-permute-start | bytes 331784 | tf_op jit(solution)/shard_map/ppermute | solution.py:496
  41.9 6.4 %collective-permute-start.4 = (f32[72,384]{1,0:T(8,128)S(1)}, f32[72,384]{1,0:T(8,128)S(1)}, u32[]{:S(2)}, u32[]{:S(2)}) collective-permute-start(f32[72,384]{1,0:T(8,128)S(1)} %get-tuple-element.18), channel_id=1, source_target_pairs={{0,3},{1,0},{2,1},{3,2},{4,7},{5,4},{6,5},{7,6},{8,11},{9,8},{10,9... | collective-permute-start | bytes 331784 | tf_op jit(solution)/shard_map/ppermute | solution.py:496
  48.3 4.8 %collective-permute-start.5 = (f32[72,384]{1,0:T(8,128)S(1)}, f32[72,384]{1,0:T(8,128)S(1)}, u32[]{:S(2)}, u32[]{:S(2)}) collective-permute-start(f32[72,384]{1,0:T(8,128)S(1)} %fusion.2), channel_id=1, source_target_pairs={{0,8},{4,12},{8,0},{12,4},{16,24},{20,28},{24,16},{28,20},{1,9},{5... | collective-permute-start | bytes 331784 | tf_op jit(solution)/shard_map/ppermute | solution.py:487
  53.2 6.9 %collective-permute-start.6 = (f32[72,384]{1,0:T(8,128)S(1)}, f32[72,384]{1,0:T(8,128)S(1)}, u32[]{:S(2)}, u32[]{:S(2)}) collective-permute-start(f32[72,384]{1,0:T(8,128)S(1)} %add.76), channel_id=1, source_target_pairs={{0,16},{4,20},{8,24},{12,28},{16,0},{20,4},{24,8},{28,12},{1,17},{... | collective-permute-start | bytes 331784 | tf_op jit(solution)/shard_map/ppermute | solution.py:487
  60.1 11.7 %collective-permute-start.7 = (f32[72,384]{1,0:T(8,128)S(1)}, f32[72,384]{1,0:T(8,128)S(1)}, u32[]{:S(2)}, u32[]{:S(2)}) collective-permute-start(f32[72,384]{1,0:T(8,128)S(1)} %add.77), channel_id=1, source_target_pairs={{0,4},{4,0},{8,12},{12,8},{16,20},{20,16},{24,28},{28,24},{1,5},{5... | collective-permute-start | bytes 331784 | tf_op jit(solution)/shard_map/ppermute | solution.py:487

commit v4 on v3

--- a/solution.py
+++ b/solution.py
@@ -43,6 +43,7 @@
 def score_table(table, conv_weight, scorer):
     return pl.pallas_call(
         score_kernel,
+        out_specs=pl.BlockSpec(memory_space=pltpu.VMEM),
         out_shape=jax.ShapeDtypeStruct((TAPS, table.shape[0]), F32),
         name="score_table",
     )(table, conv_weight, scorer)
@@ -65,12 +66,12 @@
 
 
 def main_kernel(
-    core_ref, byte_ref, seg_ref, halo_ref, table_ref, weight_ref, scorer_ref, score_ref, cot_ref,
+    byte_ref, seg_ref, halo_ref, table_ref, weight_ref, scorer_ref, score_ref, cot_ref,
     conv_ref, col_ref, mine_ref, other_ref,
-    pick_scr, gam_scr, col_scr, column_scr, keep_scr, prob_scr, rim_scr, emb_a, emb_b, mask_a, mask_b, dcol_scr, prod_scr, zeta_scr,
+    line_scr, hot_scr, col_scr, column_scr, keep_scr, prob_scr, rim_scr, emb_a, emb_b, mask_a, mask_b, dcol_scr, prod_scr, zeta_scr,
     weight_scr, mix_a, mix_b, sum_scr,
 ):
-    rows, _, padded = pick_scr.shape
+    rows, _, padded = col_scr.shape
     vocab, width = table_ref.shape
     pairs = cot_ref.shape[1]
     row = pl.program_id(0)
@@ -96,9 +97,16 @@
         for i in range(rows):
             scr[i, pl.ds(q, 1)] = value[i : i + 1]
 
+    def line(q, tile, i):
+        return (q * (padded // LANES) + tile) * rows + i
+
+    def lay(q, value):
+        for tile in range(padded // LANES):
+            line_scr[pl.ds(line(q, tile, 0), rows)] = value[:, tile * LANES : (tile + 1) * LANES]
+
     @pl.when(row == 0)
     def _():
-        halo = halo_ref[...]
+        halo = jnp.where(lax.axis_index("seq") == 0, -vocab, halo_ref[...])
         codes = jnp.concatenate(
             [
                 jnp.concatenate([halo & (vocab - 1), byte_ref[...]], axis=1),
@@ -124,9 +132,10 @@
                 keep = jnp.where(seg[parity] == back(seg[s % 2], s // 2), 1.0, 0.0)
                 keep_scr[parity * TAPS + k] = keep
                 put(col_scr, 2 + parity * (TAPS - 1) + k - 1, keep)
+        bytes_at = [back(byte[s % 2], s // 2) for s in range(SPAN)]
         byte = [b.astype(jnp.int32) for b in byte]
         for s in range(SPAN):
-            put(pick_scr, s, back(byte[s % 2], s // 2))
+            lay(s, bytes_at[s])
         found = []
         for k in range(TAPS):
             halves = [score_ref[k : k + 1, h * LANES : (h + 1) * LANES] for h in range(2)]
@@ -151,10 +160,21 @@
                 prob_scr[start * TAPS + b] = level[b]
                 share = share + level[b] * inverse[b]
                 beta[start + b] = beta[start + b] + 0.5 * keeps(start, b) * share
+        alike = {
+            (s, u): bytes_at[s] == bytes_at[u] for s in range(SPAN) for u in range(s + 1, min(s + REACH, SPAN))
+        }
         for r in range(REACH):
             put(col_scr, 2 * TAPS + r, beta[r])
-            for k in range(TAPS):
-                put(gam_scr, r * TAPS + k, beta[r] * same(r, k))
+        for k in range(TAPS):
+            alone = [beta[r] * same(r, k) for r in range(REACH)]
+            for r in range(REACH):
+                total = alone[r]
+                for u in range(REACH):
+                    if u != r:
+                        total = total + jnp.where(alike[min(r, u) + k, max(r, u) + k], alone[u], 0.0)
+                hi = total.astype(BF16).astype(F32)
+                lay(SPAN + 2 * (r * TAPS + k), hi)
+                lay(SPAN + 2 * (r * TAPS + k) + 1, total - hi)
 
     deep = HALO + pairs
     group = pairs // GROUPS
@@ -170,6 +190,8 @@
         column = column_scr[i, pl.ds(at, group)]
         value = lax.broadcasted_iota(jnp.int32, (group, vocab), 1).astype(F32)
         hot = [jnp.where(column[:, p : p + 1] == value, 1.0, 0.0).astype(BF16) for p in range(2)]
+        for p in range(2):
+            hot_scr[i, p, pl.ds(j * group, group)] = hot[p]
         found = dot(jnp.concatenate(hot, axis=0), table_ref[...])
         for p in range(2):
             for d in range(tiles):
@@ -183,19 +205,25 @@
                 embs[slot][pl.ds(to, HALO)] = rim_scr[p, d, i]
 
     def mixing(i, slot, j):
-        for lane in lanes_of(pairs):
+        deep_v = 32
+        for tile, lane in enumerate(lanes_of(pairs)):
             size = lane.size
-            byte = [pick_scr[i, pl.ds(s, 1), lane] for s in range(SPAN)]
-            gam = [gam_scr[i, pl.ds(q, 1), lane] for q in range(REACH * TAPS)]
-            base = lax.broadcasted_iota(jnp.int32, (16, size), 0) + j * part_v
-            for v in range(0, part_v, 16):
-                hit = [b == base + v for b in byte]
-                at = pl.ds(pl.multiple_of(j * part_v + v, 16), 16)
+
+            def full(q):
+                return jnp.broadcast_to(line_scr[pl.ds(line(q, tile, i), 1)][:, :size], (deep_v, size)).astype(BF16)
+
+            byte = [full(s) for s in range(SPAN)]
+            base = lax.broadcasted_iota(jnp.int32, (deep_v, size), 0).astype(F32).astype(BF16)
+            for v in range(0, part_v, deep_v):
+                value = base + (j * part_v + v)
+                hit = [b == value for b in byte]
+                at = pl.ds(j * part_v + v, deep_v)
                 for k in range(TAPS):
-                    mixed = sum(jnp.where(hit[r + k], gam[r * TAPS + k], 0.0) for r in range(REACH))
-                    hi, lo = split(mixed)
-                    mixes[slot][k, 0, at, lane] = hi
-                    mixes[slot][k, 1, at, lane] = lo
+                    for half in range(2):
+                        mixed = jnp.zeros((deep_v, size), BF16)
+                        for r in range(REACH):
+                            mixed = jnp.where(hit[r + k], full(SPAN + 2 * (r * TAPS + k) + half), mixed)
+                        mixes[slot][k, half, at, lane] = mixed
 
     def gather(slot, j, first):
         cot = cot_ref[0]
@@ -266,6 +294,9 @@
                 jnp.where(column_scr[i, pl.ds(0, HALO)][:, p : p + 1] == value, 1.0, 0.0).astype(BF16)
                 for i in range(rows)
             ]
+            for i in range(rows):
+                hot_scr[i, p, pl.ds(pairs, padded - HALO - pairs)] = jnp.zeros((padded - HALO - pairs, vocab), BF16)
+                hot_scr[i, p, pl.ds(padded - HALO, HALO)] = hot[i]
             found = dot(jnp.concatenate(hot, axis=0), table_ref[...])
             for d in range(tiles):
                 for i in range(rows):
@@ -339,25 +370,24 @@
                 for i in range(rows):
                     zeta_scr[i, parity, k : k + 1] = hi[i : i + 1]
                     zeta_scr[i, parity, TAPS + k : TAPS + k + 1] = low[i : i + 1]
-        base = lax.broadcasted_iota(jnp.int32, (vocab, padded), 0)
-
-        found = jnp.zeros((vocab, 2 * TAPS), F32)
+        found = jnp.zeros((2 * TAPS, vocab), F32)
         for i in range(rows):
-            hot = [jnp.where(pick_scr[i, pl.ds(p, 1)] == base, 1.0, 0.0).astype(BF16) for p in range(2)]
-            found = found + dot_nt(
-                jnp.concatenate(hot, axis=1),
-                jnp.concatenate([zeta_scr[i, p].astype(BF16) for p in range(2)], axis=1),
-            )
-        found = found[:, :TAPS] + found[:, TAPS:]
+            for p in range(2):
+                found = found + dot(zeta_scr[i, p].astype(BF16), hot_scr[i, p])
+        found = found[:TAPS] + found[TAPS:]
         scorer = scorer_ref[...].reshape(1, -1).astype(F32)
         weight = weight_ref[...].astype(F32)
         table = table_ref[...].astype(F32)
         hi, lo = split(found)
-        tall = lambda a, b: lax.dot_general(a, b, (((0,), (0,)), ((), ())), preferred_element_type=F32)
-        sums = tall(hi, table_ref[...]) + tall(lo, table_ref[...])
+        sums = dot(hi, table_ref[...]) + dot(lo, table_ref[...])
+        hi, lo = hi.astype(F32), lo.astype(F32)
         near, rest = split(weight * scorer)
-        grad = dot(
-            jnp.concatenate([hi, lo, hi], axis=1), jnp.concatenate([near, near, rest], axis=0)
+        near, rest = near.astype(F32), rest.astype(F32)
+        grad = lax.dot_general(
+            jnp.concatenate([hi, lo, hi], axis=0).astype(BF16),
+            jnp.concatenate([near, near, rest], axis=0).astype(BF16),
+            (((0,), (0,)), ((), ())),
+            preferred_element_type=F32,
         )
         conv, score_grad = [], 0.0
         for k in range(TAPS):
@@ -367,7 +397,7 @@
             score_grad = score_grad + weight[k : k + 1] * sums[k : k + 1]
         rest = jnp.concatenate(conv + [score_grad, jnp.zeros((8 - TAPS - 1, width), F32)], axis=0)
         half = width // 2
-        first = core_ref[0] == 0
+        first = lax.axis_index("rows") % 2 == 0
         for at, value in ((0, grad), (vocab, rest)):
             to = pl.ds(at, value.shape[0])
             left, right = value[:, :half], value[:, half:]
@@ -421,7 +451,7 @@
     )(*[conv] * (2 * STREAMS), columns, *([] if before is None else [before]))
 
 
-def main(core, byte_ids, segment_ids, halo, table, conv_weight, scorer, scores, cotangent):
+def main(byte_ids, segment_ids, halo, table, conv_weight, scorer, scores, cotangent):
     rows, pairs, width = cotangent.shape
     vocab = table.shape[0]
     assert rows * 8 <= LANES
@@ -432,21 +462,20 @@
         main_kernel,
         grid=(rows,),
         in_specs=[
-            pl.BlockSpec(memory_space=pltpu.SMEM),
             whole(byte_ids.shape),
             whole(segment_ids.shape),
-            whole(halo.shape),
+            pl.BlockSpec(memory_space=pltpu.VMEM),
             whole((vocab, width)),
             whole((TAPS, width)),
             whole((width,)),
-            whole((TAPS, vocab)),
+            pl.BlockSpec(memory_space=pltpu.VMEM),
             pl.BlockSpec((1, pairs, width), lambda i: (i, 0, 0)),
         ],
         out_specs=[
             pl.BlockSpec((None, 2 * tiles * (HALO + pairs), LANES), lambda i: (i, 0, 0)),
             whole((rows, 16, padded)),
-            whole((vocab + 8, width // 2)),
-            whole((vocab + 8, width // 2)),
+            pl.BlockSpec(memory_space=pltpu.VMEM),
+            pl.BlockSpec(memory_space=pltpu.VMEM),
         ],
         out_shape=[
             jax.ShapeDtypeStruct((rows, 2 * tiles * (HALO + pairs), LANES), F32),
@@ -455,8 +484,8 @@
             jax.ShapeDtypeStruct((vocab + 8, width // 2), F32),
         ],
         scratch_shapes=[
-            pltpu.VMEM((rows, SPAN, padded), jnp.int32),
-            pltpu.VMEM((rows, REACH * TAPS, padded), F32),
+            pltpu.VMEM(((SPAN + 2 * REACH * TAPS) * padded // LANES * rows, LANES), F32),
+            pltpu.VMEM((rows, 2, padded, vocab), BF16),
             pltpu.VMEM((rows, 16, padded), F32),
             pltpu.VMEM((rows, HALO + pairs, 16), F32),
             pltpu.VMEM((2 * TAPS, rows, padded), F32),
@@ -475,7 +504,7 @@
             pltpu.VMEM((TAPS * vocab, width), F32),
         ],
         name="main",
-    )(core, byte_ids, segment_ids, halo, table, conv_weight, scorer, scores, cotangent)
+    )(byte_ids, segment_ids, halo, table, conv_weight, scorer, scores, cotangent)
 
 
 def add_parts(mine, other, rows_axis, seq_axis, vocab):
@@ -511,11 +540,11 @@
     rows, pairs, width = cotangent.shape
     tail = byte_ids[:, -LANES:] + vocab * segment_ids[:, -LANES:]
     halo = lax.ppermute(tail, "seq", [(i, i + 1) for i in range(parts - 1)])
-    halo = jnp.where(lax.axis_index("seq") == 0, -vocab, halo)
-    core = (lax.axis_index("rows") % 2)[None]
     scores = score_table(table, conv_weight, scorer)
-    conv, columns, mine, other = main(core, byte_ids, segment_ids, halo, table, conv_weight, scorer, scores, cotangent)
-    cuts = (0, rows // 2, rows - rows // 4, rows)
+    conv, columns, mine, other = main(
+        byte_ids, segment_ids, halo, table, conv_weight, scorer, scores, cotangent
+    )
+    cuts = (0, rows * 3 // 8, rows * 5 // 8, rows)
     out = None
     for n in range(3):
         out = blocks(conv, columns, pairs, width, cuts[n], cuts[n + 1], out)

time: 74 us -> 72.9 us (0.985)
  Pallas kernels: 40.4 us -> 39.2 us
    pallas_call x2, Pallas kernels: 28.8 us -> 26.6 us  [the longest x1 24.7 us: main(): pl.pallas_call(main_kernel, grid=(rows,), in_specs=[whole(byte_ids.shape)...]
    pallas_call x3, Pallas kernels: 11.6 us -> 12.6 us  [blocks(): pl.pallas_call(blocks_kernel, grid=(stop - start,), in_specs=[part(n) for...]
  transfers between devices with their start and end apart: 8 -> 8, of which waited for: 6 -> 6; matrix products, arithmetic and copies ran while one was open for 0% -> 0% of each run, Pallas kernels for 18% -> 20%
where the time goes in v4:
time: 72.9 us; the launch traced here: 72.5 us
  Pallas kernels  39.2 us (54%)
  starting transfers between devices  14.8 us (20%)
  waiting for transfers between devices  13.3 us (18%)
  local copies, waits for them, and re-layouts  2.54 us (3%)
  other arithmetic  1.87 us (3%)
  between operations  0.77 us (1%)
    pallas_call x1, Pallas kernels, main(): pl.pallas_call(main_kernel, grid=(rows,), in_specs=[whole(byte_ids.shape)...  24.7 us
    pallas_call x3, Pallas kernels, blocks(): pl.pallas_call(blocks_kernel, grid=(stop - start,), in_specs=[part(n) for...  12.6 us
    ppermute x4, waiting for transfers between devices, swap(): return lax.ppermute(x, rows_axis, [(i, i ^ stride) for i in range(ranks)])  9.3 us
    ppermute x3, starting transfers between devices, add_parts(): lax.ppermute(piece(n), seq_axis, [(i, (i + n) % parts) for i in range(par...  5.56 us
    ppermute x1, starting transfers between devices, per_device(): halo = lax.ppermute(tail, 'seq', [(i, i + 1) for i in range(parts - 1)])  4.86 us
    ppermute x4, starting transfers between devices, swap(): return lax.ppermute(x, rows_axis, [(i, i ^ stride) for i in range(ranks)])  4.37 us
    ppermute x3, waiting for transfers between devices, add_parts(): lax.ppermute(piece(n), seq_axis, [(i, (i + n) % parts) for i in range(par...  4.03 us
    pallas_call x1, Pallas kernels, score_table(): pl.pallas_call(score_kernel, out_specs=pl.BlockSpec(memory_space=pltpu.VM...  1.93 us
  transfers between devices with their start and end apart: 8, of which 6 were waited for; matrix products, arithmetic and copies ran while one was open for 0% of the time, Pallas kernels for 20%

profile of v4, /device:TPU:0, one launch (start us, length us, event | category | flops | bytes accessed | tf_op | source)
XLA Modules:
  0.0 72.5 jit_solution(1245779727182396873)
XLA Ops:
  0.6 0.7 multiply_add_fusion
  1.3 4.9 %collective-permute-start = (s32[8,128]{1,0:T(8,128)S(1)}, s32[8,128]{1,0:T(8,128)S(1)}, u32[]{:S(2)}, u32[]{:S(2)}) collective-permute-start(s32[8,128]{1,0:T(8,128)S(1)} %multiply_add_fusion), channel_id=1, source_target_pairs={{0,1},{1,2},{2,3},{4,5},{5,6},{6,7},{8,9},{9,10},{10,11},{12,13},{... | collective-permute-start | bytes 12296 | tf_op jit(solution)/shard_map/ppermute | solution.py:542
  6.2 1.9 %score_table.1.score_ref = f32[4,256]{1,0:T(4,128)} custom-call(bf16[256,768]{1,0:T(8,128)(2,1)} %table_ref.3, bf16[4,768]{1,0:T(4,128)(2,1)} %weight_ref.3, bf16[768]{0:T(1024)(128)(2,1)} %scorer_ref.3), custom_call_target="tpu_custom_call" | custom-call | tf_op jit(solution)/shard_map/score_table/pallas_call | solution.py:44
  8.1 0.0 collective-permute-done.halo_ref
  8.1 0.0 copy-start
  8.1 0.6 copy-done
  8.7 24.7 %main.1 = (f32[8,3264,128]{2,1,0:T(8,128)}, f32[8,16,384]{2,1,0:T(8,128)}, f32[264,384]{1,0:T(8,128)}, f32[264,384]{1,0:T(8,128)}) custom-call(s32[8,512]{1,0:T(8,128)} %byte_ref.1, s32[8,512]{1,0:T(8,128)} %seg_ref.1, s32[8,128]{1,0:T(8,128)} %copy-done, bf16[256,768]{1,0:T(8,128)(2,1)} %table_ref.3, bf16[4,768]{1,0:T(4,128)(2,1)} %weight_ref.3, ...), custom_call_target="tpu_custom_call" | custom-call | tf_op jit(solution)/shard_map/main/pallas_call | solution.py:461
  33.5 0.0 collective-permute-start.1
  33.5 1.9 %collective-permute-done.1 = f32[264,384]{1,0:T(8,128)S(1)} collective-permute-done((f32[264,384]{1,0:T(8,128)}, f32[264,384]{1,0:T(8,128)S(1)}, u32[]{:S(2)}, u32[]{:S(2)}) %collective-permute-start.1) | collective-permute-done | bytes 405536 | tf_op jit(solution)/shard_map/ppermute | solution.py:516
  35.4 1.0 %add.60 = f32[264,384]{1,0:T(8,128)S(1)} add(f32[264,384]{1,0:T(8,128)} %get-tuple-element.10, f32[264,384]{1,0:T(8,128)S(1)} %collective-permute-done.1) | non-fusion elementwise | flops 101376 | bytes 1216512 | tf_op jit(solution)/shard_map/add | solution.py:518
  36.5 1.7 %collective-permute-start.2 = (f32[72,384]{1,0:T(8,128)S(1)}, f32[72,384]{1,0:T(8,128)S(1)}, u32[]{:S(2)}, u32[]{:S(2)}) collective-permute-start(f32[72,384]{1,0:T(8,128)S(1)} %get-tuple-element.16), channel_id=1, source_target_pairs={{0,1},{1,2},{2,3},{3,0},{4,5},{5,6},{6,7},{7,4},{8,9},{9,10},{10,1... | collective-permute-start | bytes 331784 | tf_op jit(solution)/shard_map/ppermute | solution.py:525
  38.3 1.5 %collective-permute-start.3 = (f32[72,384]{1,0:T(8,128)S(1)}, f32[72,384]{1,0:T(8,128)S(1)}, u32[]{:S(2)}, u32[]{:S(2)}) collective-permute-start(f32[72,384]{1,0:T(8,128)S(1)} %get-tuple-element.17), channel_id=1, source_target_pairs={{0,2},{1,3},{2,0},{3,1},{4,6},{5,7},{6,4},{7,5},{8,10},{9,11},{10,... | collective-permute-start | bytes 331784 | tf_op jit(solution)/shard_map/ppermute | solution.py:525
  39.8 2.3 %collective-permute-start.4 = (f32[72,384]{1,0:T(8,128)S(1)}, f32[72,384]{1,0:T(8,128)S(1)}, u32[]{:S(2)}, u32[]{:S(2)}) collective-permute-start(f32[72,384]{1,0:T(8,128)S(1)} %get-tuple-element.18), channel_id=1, source_target_pairs={{0,3},{1,0},{2,1},{3,2},{4,7},{5,4},{6,5},{7,6},{8,11},{9,8},{10,9... | collective-permute-start | bytes 331784 | tf_op jit(solution)/shard_map/ppermute | solution.py:525
  42.1 0.6 collective-permute-done.2
  42.7 2.2 %collective-permute-done.3 = f32[72,384]{1,0:T(8,128)S(1)} collective-permute-done((f32[72,384]{1,0:T(8,128)S(1)}, f32[72,384]{1,0:T(8,128)S(1)}, u32[]{:S(2)}, u32[]{:S(2)}) %collective-permute-start.3) | collective-permute-done | bytes 110624 | tf_op jit(solution)/shard_map/ppermute | solution.py:525
  45.0 1.2 %collective-permute-done.4 = f32[72,384]{1,0:T(8,128)S(1)} collective-permute-done((f32[72,384]{1,0:T(8,128)S(1)}, f32[72,384]{1,0:T(8,128)S(1)}, u32[]{:S(2)}, u32[]{:S(2)}) %collective-permute-start.4) | collective-permute-done | bytes 110624 | tf_op jit(solution)/shard_map/ppermute | solution.py:525
  46.2 1.6 %collective-permute-start.5 = (f32[72,384]{1,0:T(8,128)S(1)}, f32[72,384]{1,0:T(8,128)S(1)}, u32[]{:S(2)}, u32[]{:S(2)}) collective-permute-start(f32[72,384]{1,0:T(8,128)S(1)} %fusion.2), channel_id=1, source_target_pairs={{0,8},{4,12},{8,0},{12,4},{16,24},{20,28},{24,16},{28,20},{1,9},{5... | collective-permute-start | bytes 331784 | tf_op jit(solution)/shard_map/ppermute | solution.py:516
  47.8 3.2 %collective-permute-done.5 = f32[72,384]{1,0:T(8,128)S(1)} collective-permute-done((f32[72,384]{1,0:T(8,128)S(1)}, f32[72,384]{1,0:T(8,128)S(1)}, u32[]{:S(2)}, u32[]{:S(2)}) %collective-permute-start.5) | collective-permute-done | bytes 110624 | tf_op jit(solution)/shard_map/ppermute | solution.py:516
  51.0 2.7 %collective-permute-start.6 = (f32[72,384]{1,0:T(8,128)S(1)}, f32[72,384]{1,0:T(8,128)S(1)}, u32[]{:S(2)}, u32[]{:S(2)}) collective-permute-start(f32[72,384]{1,0:T(8,128)S(1)} %add.75), channel_id=1, source_target_pairs={{0,16},{4,20},{8,24},{12,28},{16,0},{20,4},{24,8},{28,12},{1,17},{... | collective-permute-start | bytes 331784 | tf_op jit(solution)/shard_map/ppermute | solution.py:516
  53.7 4.2 %collective-permute-done.6 = f32[72,384]{1,0:T(8,128)S(1)} collective-permute-done((f32[72,384]{1,0:T(8,128)S(1)}, f32[72,384]{1,0:T(8,128)S(1)}, u32[]{:S(2)}, u32[]{:S(2)}) %collective-permute-start.6) | collective-permute-done | bytes 110624 | tf_op jit(solution)/shard_map/ppermute | solution.py:516
  57.9 0.1 collective-permute-start.7
  58.0 4.7 %blocks.3.refs_7_ = bf16[8,256,768]{2,1,0:T(8,128)(2,1)} custom-call(f32[8,6,544,128]{3,2,1,0:T(8,128)} %bitcast.1, f32[8,6,544,128]{3,2,1,0:T(8,128)} %bitcast.2, f32[8,6,544,128]{3,2,1,0:T(8,128)} %bitcast.3, f32[8,6,544,128]{3,2,1,0:T(8,128)} %bitcast.4, f32[8,6,544,128]{3,2,1,0:T(8,128)} %bitcast.5, f32[8,6,544,128]{3,2,1,0:T(8,128)} %bitcast.6, ...), custom_call_target="tpu_custom_call" | custom-call | flops 5308416 | bytes 6193152 | tf_op jit(solution)/shard_map/blocks/pallas_call | solution.py:436
  62.7 3.1 %blocks.4.refs_7_ = bf16[8,256,768]{2,1,0:T(8,128)(2,1)} custom-call(f32[8,6,544,128]{3,2,1,0:T(8,128)} %bitcast.7, f32[8,6,544,128]{3,2,1,0:T(8,128)} %bitcast.8, f32[8,6,544,128]{3,2,1,0:T(8,128)} %bitcast.9, f32[8,6,544,128]{3,2,1,0:T(8,128)} %bitcast.10, f32[8,6,544,128]{3,2,1,0:T(8,128)} %bitcast.11, ...), custom_call_target="tpu_custom_call", output_to_operand_aliasing={{}: (7, {})} | custom-call | flops 3538944 | bytes 4128768 | tf_op jit(solution)/shard_map/blocks/pallas_call | solution.py:436
  65.8 4.7 %blocks.5 = bf16[8,256,768]{2,1,0:T(8,128)(2,1)} custom-call(f32[8,6,544,128]{3,2,1,0:T(8,128)} %bitcast.13, f32[8,6,544,128]{3,2,1,0:T(8,128)} %bitcast.14, f32[8,6,544,128]{3,2,1,0:T(8,128)} %bitcast.15, f32[8,6,544,128]{3,2,1,0:T(8,128)} %bitcast.16, f32[8,6,544,128]{3,2,1,0:T(8,128)} %bitcast.17, ...), custom_call_target="tpu_custom_call", output_to_operand_aliasing={{}: (7, {})} | custom-call | flops 5308416 | bytes 6193152 | tf_op jit(solution)/shard_map/blocks/pallas_call | solution.py:436
  70.6 0.0 collective-permute-done.7
  70.6 0.6 slice_reduce_fusion
  71.2 0.6 slice.26
  71.8 0.7 slice.25
  (7 shorter events, 0.2 us)
Async XLA Ops:
  1.3 6.8 %collective-permute-start = (s32[8,128]{1,0:T(8,128)S(1)}, s32[8,128]{1,0:T(8,128)S(1)}, u32[]{:S(2)}, u32[]{:S(2)}) collective-permute-start(s32[8,128]{1,0:T(8,128)S(1)} %multiply_add_fusion), channel_id=1, source_target_pairs={{0,1},{1,2},{2,3},{4,5},{5,6},{6,7},{8,9},{9,10},{10,11},{12,13},{... | collective-permute-start | bytes 12296 | tf_op jit(solution)/shard_map/ppermute | solution.py:542
  8.1 0.6 copy-start
  33.5 2.0 %collective-permute-start.1 = (f32[264,384]{1,0:T(8,128)}, f32[264,384]{1,0:T(8,128)S(1)}, u32[]{:S(2)}, u32[]{:S(2)}) collective-permute-start(f32[264,384]{1,0:T(8,128)} %get-tuple-element.11), channel_id=1, source_target_pairs={{0,4},{4,0},{8,12},{12,8},{16,20},{20,16},{24,28},{28,24},{1,5},{5... | collective-permute-start | bytes 1216520 | tf_op jit(solution)/shard_map/ppermute | solution.py:516
  36.5 6.2 %collective-permute-start.2 = (f32[72,384]{1,0:T(8,128)S(1)}, f32[72,384]{1,0:T(8,128)S(1)}, u32[]{:S(2)}, u32[]{:S(2)}) collective-permute-start(f32[72,384]{1,0:T(8,128)S(1)} %get-tuple-element.16), channel_id=1, source_target_pairs={{0,1},{1,2},{2,3},{3,0},{4,5},{5,6},{6,7},{7,4},{8,9},{9,10},{10,1... | collective-permute-start | bytes 331784 | tf_op jit(solution)/shard_map/ppermute | solution.py:525
  38.3 6.7 %collective-permute-start.3 = (f32[72,384]{1,0:T(8,128)S(1)}, f32[72,384]{1,0:T(8,128)S(1)}, u32[]{:S(2)}, u32[]{:S(2)}) collective-permute-start(f32[72,384]{1,0:T(8,128)S(1)} %get-tuple-element.17), channel_id=1, source_target_pairs={{0,2},{1,3},{2,0},{3,1},{4,6},{5,7},{6,4},{7,5},{8,10},{9,11},{10,... | collective-permute-start | bytes 331784 | tf_op jit(solution)/shard_map/ppermute | solution.py:525
  39.8 6.4 %collective-permute-start.4 = (f32[72,384]{1,0:T(8,128)S(1)}, f32[72,384]{1,0:T(8,128)S(1)}, u32[]{:S(2)}, u32[]{:S(2)}) collective-permute-start(f32[72,384]{1,0:T(8,128)S(1)} %get-tuple-element.18), channel_id=1, source_target_pairs={{0,3},{1,0},{2,1},{3,2},{4,7},{5,4},{6,5},{7,6},{8,11},{9,8},{10,9... | collective-permute-start | bytes 331784 | tf_op jit(solution)/shard_map/ppermute | solution.py:525
  46.2 4.8 %collective-permute-start.5 = (f32[72,384]{1,0:T(8,128)S(1)}, f32[72,384]{1,0:T(8,128)S(1)}, u32[]{:S(2)}, u32[]{:S(2)}) collective-permute-start(f32[72,384]{1,0:T(8,128)S(1)} %fusion.2), channel_id=1, source_target_pairs={{0,8},{4,12},{8,0},{12,4},{16,24},{20,28},{24,16},{28,20},{1,9},{5... | collective-permute-start | bytes 331784 | tf_op jit(solution)/shard_map/ppermute | solution.py:516
  51.0 6.9 %collective-permute-start.6 = (f32[72,384]{1,0:T(8,128)S(1)}, f32[72,384]{1,0:T(8,128)S(1)}, u32[]{:S(2)}, u32[]{:S(2)}) collective-permute-start(f32[72,384]{1,0:T(8,128)S(1)} %add.75), channel_id=1, source_target_pairs={{0,16},{4,20},{8,24},{12,28},{16,0},{20,4},{24,8},{28,12},{1,17},{... | collective-permute-start | bytes 331784 | tf_op jit(solution)/shard_map/ppermute | solution.py:516
  57.9 12.7 %collective-permute-start.7 = (f32[72,384]{1,0:T(8,128)S(1)}, f32[72,384]{1,0:T(8,128)S(1)}, u32[]{:S(2)}, u32[]{:S(2)}) collective-permute-start(f32[72,384]{1,0:T(8,128)S(1)} %add.76), channel_id=1, source_target_pairs={{0,4},{4,0},{8,12},{12,8},{16,20},{20,16},{24,28},{28,24},{1,5},{5... | collective-permute-start | bytes 331784 | tf_op jit(solution)/shard_map/ppermute | solution.py:516

commit v5 on v4

--- a/solution.py
+++ b/solution.py
@@ -33,20 +33,6 @@
 def lanes_of(width):
     step = min(width, LANES)
     return [pl.ds(at, step) for at in range(0, width, step)]
-
-
-def score_kernel(table_ref, weight_ref, scorer_ref, score_ref):
-    hi, lo = split(weight_ref[...].astype(F32) * scorer_ref[...].reshape(1, -1).astype(F32))
-    score_ref[...] = dot_nt(hi, table_ref[...]) + dot_nt(lo, table_ref[...])
-
-
-def score_table(table, conv_weight, scorer):
-    return pl.pallas_call(
-        score_kernel,
-        out_specs=pl.BlockSpec(memory_space=pltpu.VMEM),
-        out_shape=jax.ShapeDtypeStruct((TAPS, table.shape[0]), F32),
-        name="score_table",
-    )(table, conv_weight, scorer)
 
 
 def look_up(rows_of, index):
@@ -62,11 +48,12 @@
 
 
 HALO = 16
+UNITS = 1
 GROUPS = 1
 
 
 def main_kernel(
-    byte_ref, seg_ref, halo_ref, table_ref, weight_ref, scorer_ref, score_ref, cot_ref,
+    byte_ref, seg_ref, halo_ref, table_ref, weight_ref, scorer_ref, cot_ref,
     conv_ref, col_ref, mine_ref, other_ref,
     line_scr, hot_scr, col_scr, column_scr, keep_scr, prob_scr, rim_scr, emb_a, emb_b, mask_a, mask_b, dcol_scr, prod_scr, zeta_scr,
     weight_scr, mix_a, mix_b, sum_scr,
@@ -137,8 +124,10 @@
         for s in range(SPAN):
             lay(s, bytes_at[s])
         found = []
+        hi, lo = split(weight_ref[...].astype(F32) * scorer_ref[...].reshape(1, -1).astype(F32))
+        scores = dot_nt(hi, table_ref[...]) + dot_nt(lo, table_ref[...])
         for k in range(TAPS):
-            halves = [score_ref[k : k + 1, h * LANES : (h + 1) * LANES] for h in range(2)]
+            halves = [scores[k : k + 1, h * LANES : (h + 1) * LANES] for h in range(2)]
             found.append([look_up(halves, byte[parity]) for parity in range(2)])
         scored = [
             sum(keeps(parity, k) * back(found[k][(parity + k) % 2], (parity + k) // 2) for k in range(TAPS))
@@ -246,23 +235,29 @@
                 place = pl.multiple_of(q * (8 + pairs) + to + t, 8)
                 masks[slot][pl.ds(place, 8)] = jnp.broadcast_to(column[:, 2 + q : 3 + q], (8, LANES))
 
-    def conved(slot, at):
+    def conved(slot, places):
         keep = [
-            masks[slot][pl.ds(pl.multiple_of(q * (8 + pairs) + at - HALO + 8, 8), 8)] for q in range(2 * (TAPS - 1))
+            [masks[slot][pl.ds(pl.multiple_of(q * (8 + pairs) + at - HALO + 8, 8), 8)] for q in range(2 * (TAPS - 1))]
+            for at in places
         ]
         for d in range(tiles):
-            taken = [embs[slot][pl.ds(spot(s % 2, d) + at - s // 2, 8)] for s in range(REACH)]
-            for p in range(2):
-                total = weight_scr[0, d] * taken[p]
-                for k in range(1, TAPS):
-                    total = total + keep[p * (TAPS - 1) + k - 1] * (weight_scr[k, d] * taken[p + k])
+            weight = [weight_scr[k, d] for k in range(TAPS)]
+            ready = []
+            for n, at in enumerate(places):
+                taken = [embs[slot][pl.ds(spot(s % 2, d) + at - s // 2, 8)] for s in range(REACH)]
+                for p in range(2):
+                    total = weight[0] * taken[p]
+                    for k in range(1, TAPS):
+                        total = total + keep[n][p * (TAPS - 1) + k - 1] * (weight[k] * taken[p + k])
+                    ready.append((p, at, total))
+            for p, at, total in ready:
                 conv_ref[pl.ds(pl.multiple_of(spot(p, d) + at, 8), 8)] = total
 
     lane_at = lax.broadcasted_iota(jnp.int32, (8, LANES), 1) - 8 * row
 
     def convolve(slot, j):
-        for t in range(0, group, 8):
-            conved(slot, pl.multiple_of(HALO + j * group + t, 8))
+        for t in range(0, group, 8 * UNITS):
+            conved(slot, [pl.multiple_of(HALO + j * group + t + 8 * u, 8) for u in range(UNITS)])
 
     def products(j):
         for t in range(0, group, 16):
@@ -320,7 +315,7 @@
         if more:
             embed_rim(row + 1, 1 - slot)
             spread(row + 1, 1 - slot, HALO - 8, 0, 8)
-        conved(slot, HALO - 8)
+        conved(slot, [HALO - 8])
 
         @pl.loop(0, GROUPS)
         def _(j):
@@ -451,7 +446,7 @@
     )(*[conv] * (2 * STREAMS), columns, *([] if before is None else [before]))
 
 
-def main(byte_ids, segment_ids, halo, table, conv_weight, scorer, scores, cotangent):
+def main(byte_ids, segment_ids, halo, table, conv_weight, scorer, cotangent):
     rows, pairs, width = cotangent.shape
     vocab = table.shape[0]
     assert rows * 8 <= LANES
@@ -468,7 +463,6 @@
             whole((vocab, width)),
             whole((TAPS, width)),
             whole((width,)),
-            pl.BlockSpec(memory_space=pltpu.VMEM),
             pl.BlockSpec((1, pairs, width), lambda i: (i, 0, 0)),
         ],
         out_specs=[
@@ -504,7 +498,7 @@
             pltpu.VMEM((TAPS * vocab, width), F32),
         ],
         name="main",
-    )(byte_ids, segment_ids, halo, table, conv_weight, scorer, scores, cotangent)
+    )(byte_ids, segment_ids, halo, table, conv_weight, scorer, cotangent)
 
 
 def add_parts(mine, other, rows_axis, seq_axis, vocab):
@@ -540,13 +534,12 @@
     rows, pairs, width = cotangent.shape
     tail = byte_ids[:, -LANES:] + vocab * segment_ids[:, -LANES:]
     halo = lax.ppermute(tail, "seq", [(i, i + 1) for i in range(parts - 1)])
-    scores = score_table(table, conv_weight, scorer)
     conv, columns, mine, other = main(
-        byte_ids, segment_ids, halo, table, conv_weight, scorer, scores, cotangent
+        byte_ids, segment_ids, halo, table, conv_weight, scorer, cotangent
     )
-    cuts = (0, rows * 3 // 8, rows * 5 // 8, rows)
+    cuts = (0, rows // 8, rows * 3 // 8, rows * 5 // 8, rows)
     out = None
-    for n in range(3):
+    for n in range(4):
         out = blocks(conv, columns, pairs, width, cuts[n], cuts[n + 1], out)
     table_grad, conv_grad, scorer_grad = add_parts(mine, other, "rows", "seq", vocab)
     return (out, table_grad, conv_grad, scorer_grad)

time: 72.9 us -> 74.1 us (1.016)
  waiting for transfers between devices: 13.3 us -> 14.6 us
    pallas_call x1 -> x0, Pallas kernels: 1.93 us -> none  [score_table(): pl.pallas_call(score_kernel, out_specs=pl.BlockSpec(memory_space=pltpu.VM...]
    ppermute x1, waiting for transfers between devices: 0.01 us -> 1.31 us  [per_device(): halo = lax.ppermute(tail, 'seq', [(i, i + 1) for i in range(parts - 1)])]
    pallas_call x3 -> x4, Pallas kernels: 12.6 us -> 13.5 us  [blocks(): pl.pallas_call(blocks_kernel, grid=(stop - start,), in_specs=[part(n) for...]
  transfers between devices with their start and end apart: 8 -> 8, of which waited for: 6 -> 7; matrix products, arithmetic and copies ran while one was open for 0% -> 0% of each run, Pallas kernels for 20% -> 18%
where the time goes in v5:
time: 74.1 us; the launch traced here: 73.7 us
  Pallas kernels  38.5 us (52%)
  starting transfers between devices  15.4 us (21%)
  waiting for transfers between devices  14.6 us (20%)
  local copies, waits for them, and re-layouts  2.53 us (3%)
  other arithmetic  1.87 us (3%)
  between operations  0.77 us (1%)
    pallas_call x1, Pallas kernels, main(): pl.pallas_call(main_kernel, grid=(rows,), in_specs=[whole(byte_ids.shape)...  25 us
    pallas_call x4, Pallas kernels, blocks(): pl.pallas_call(blocks_kernel, grid=(stop - start,), in_specs=[part(n) for...  13.5 us
    ppermute x4, waiting for transfers between devices, swap(): return lax.ppermute(x, rows_axis, [(i, i ^ stride) for i in range(ranks)])  9.3 us
    ppermute x3, starting transfers between devices, add_parts(): lax.ppermute(piece(n), seq_axis, [(i, (i + n) % parts) for i in range(par...  6.18 us
    ppermute x1, starting transfers between devices, per_device(): halo = lax.ppermute(tail, 'seq', [(i, i + 1) for i in range(parts - 1)])  4.86 us
    ppermute x4, starting transfers between devices, swap(): return lax.ppermute(x, rows_axis, [(i, i ^ stride) for i in range(ranks)])  4.37 us
    ppermute x3, waiting for transfers between devices, add_parts(): lax.ppermute(piece(n), seq_axis, [(i, (i + n) % parts) for i in range(par...  4.02 us
    slice x3, local copies, waits for them, and re-layouts, add_parts(): return (whole[:share], whole[share:share + TAPS], whole[share + TAPS])  1.9 us
  transfers between devices with their start and end apart: 8, of which 7 were waited for; matrix products, arithmetic and copies ran while one was open for 0% of the time, Pallas kernels for 18%

profile of v5, /device:TPU:0, one launch (start us, length us, event | category | flops | bytes accessed | tf_op | source)
XLA Modules:
  0.0 73.7 jit_solution(14424765842508687483)
XLA Ops:
  0.6 0.7 multiply_add_fusion
  1.3 4.9 %collective-permute-start = (s32[8,128]{1,0:T(8,128)S(1)}, s32[8,128]{1,0:T(8,128)S(1)}, u32[]{:S(2)}, u32[]{:S(2)}) collective-permute-start(s32[8,128]{1,0:T(8,128)S(1)} %multiply_add_fusion), channel_id=1, source_target_pairs={{0,1},{1,2},{2,3},{4,5},{5,6},{6,7},{8,9},{9,10},{10,11},{12,13},{... | collective-permute-start | bytes 12296 | tf_op jit(solution)/shard_map/ppermute | solution.py:536
  6.2 1.3 %collective-permute-done.halo_ref = s32[8,128]{1,0:T(8,128)S(1)} collective-permute-done((s32[8,128]{1,0:T(8,128)S(1)}, s32[8,128]{1,0:T(8,128)S(1)}, u32[]{:S(2)}, u32[]{:S(2)}) %collective-permute-start) | collective-permute-done | bytes 4128 | tf_op jit(solution)/shard_map/ppermute | solution.py:536
  7.5 0.0 copy-start
  7.5 0.6 copy-done
  8.1 25.0 %main.1 = (f32[8,3264,128]{2,1,0:T(8,128)}, f32[8,16,384]{2,1,0:T(8,128)}, f32[264,384]{1,0:T(8,128)}, f32[264,384]{1,0:T(8,128)}) custom-call(s32[8,512]{1,0:T(8,128)} %byte_ref.1, s32[8,512]{1,0:T(8,128)} %seg_ref.1, s32[8,128]{1,0:T(8,128)} %copy-done, bf16[256,768]{1,0:T(8,128)(2,1)} %table_ref.1, bf16[4,768]{1,0:T(4,128)(2,1)} %weight_ref.1, ...), custom_call_target="tpu_custom_call" | custom-call | tf_op jit(solution)/shard_map/main/pallas_call | solution.py:456
  33.1 0.0 collective-permute-start.1
  33.2 1.9 %collective-permute-done.1 = f32[264,384]{1,0:T(8,128)S(1)} collective-permute-done((f32[264,384]{1,0:T(8,128)}, f32[264,384]{1,0:T(8,128)S(1)}, u32[]{:S(2)}, u32[]{:S(2)}) %collective-permute-start.1) | collective-permute-done | bytes 405536 | tf_op jit(solution)/shard_map/ppermute | solution.py:510
  35.1 1.0 %add.60 = f32[264,384]{1,0:T(8,128)S(1)} add(f32[264,384]{1,0:T(8,128)} %get-tuple-element.10, f32[264,384]{1,0:T(8,128)S(1)} %collective-permute-done.1) | non-fusion elementwise | flops 101376 | bytes 1216512 | tf_op jit(solution)/shard_map/add | solution.py:512
  36.2 2.3 %collective-permute-start.2 = (f32[72,384]{1,0:T(8,128)S(1)}, f32[72,384]{1,0:T(8,128)S(1)}, u32[]{:S(2)}, u32[]{:S(2)}) collective-permute-start(f32[72,384]{1,0:T(8,128)S(1)} %get-tuple-element.16), channel_id=1, source_target_pairs={{0,1},{1,2},{2,3},{3,0},{4,5},{5,6},{6,7},{7,4},{8,9},{9,10},{10,1... | collective-permute-start | bytes 331784 | tf_op jit(solution)/shard_map/ppermute | solution.py:519
  38.5 1.5 %collective-permute-start.3 = (f32[72,384]{1,0:T(8,128)S(1)}, f32[72,384]{1,0:T(8,128)S(1)}, u32[]{:S(2)}, u32[]{:S(2)}) collective-permute-start(f32[72,384]{1,0:T(8,128)S(1)} %get-tuple-element.17), channel_id=1, source_target_pairs={{0,2},{1,3},{2,0},{3,1},{4,6},{5,7},{6,4},{7,5},{8,10},{9,11},{10,... | collective-permute-start | bytes 331784 | tf_op jit(solution)/shard_map/ppermute | solution.py:519
  40.1 2.3 %collective-permute-start.4 = (f32[72,384]{1,0:T(8,128)S(1)}, f32[72,384]{1,0:T(8,128)S(1)}, u32[]{:S(2)}, u32[]{:S(2)}) collective-permute-start(f32[72,384]{1,0:T(8,128)S(1)} %get-tuple-element.18), channel_id=1, source_target_pairs={{0,3},{1,0},{2,1},{3,2},{4,7},{5,4},{6,5},{7,6},{8,11},{9,8},{10,9... | collective-permute-start | bytes 331784 | tf_op jit(solution)/shard_map/ppermute | solution.py:519
  42.4 0.6 collective-permute-done.2
  43.0 2.3 %collective-permute-done.3 = f32[72,384]{1,0:T(8,128)S(1)} collective-permute-done((f32[72,384]{1,0:T(8,128)S(1)}, f32[72,384]{1,0:T(8,128)S(1)}, u32[]{:S(2)}, u32[]{:S(2)}) %collective-permute-start.3) | collective-permute-done | bytes 110624 | tf_op jit(solution)/shard_map/ppermute | solution.py:519
  45.2 1.2 %collective-permute-done.4 = f32[72,384]{1,0:T(8,128)S(1)} collective-permute-done((f32[72,384]{1,0:T(8,128)S(1)}, f32[72,384]{1,0:T(8,128)S(1)}, u32[]{:S(2)}, u32[]{:S(2)}) %collective-permute-start.4) | collective-permute-done | bytes 110624 | tf_op jit(solution)/shard_map/ppermute | solution.py:519
  46.5 1.6 %collective-permute-start.5 = (f32[72,384]{1,0:T(8,128)S(1)}, f32[72,384]{1,0:T(8,128)S(1)}, u32[]{:S(2)}, u32[]{:S(2)}) collective-permute-start(f32[72,384]{1,0:T(8,128)S(1)} %fusion.2), channel_id=1, source_target_pairs={{0,8},{4,12},{8,0},{12,4},{16,24},{20,28},{24,16},{28,20},{1,9},{5... | collective-permute-start | bytes 331784 | tf_op jit(solution)/shard_map/ppermute | solution.py:510
  48.1 3.2 %collective-permute-done.5 = f32[72,384]{1,0:T(8,128)S(1)} collective-permute-done((f32[72,384]{1,0:T(8,128)S(1)}, f32[72,384]{1,0:T(8,128)S(1)}, u32[]{:S(2)}, u32[]{:S(2)}) %collective-permute-start.5) | collective-permute-done | bytes 110624 | tf_op jit(solution)/shard_map/ppermute | solution.py:510
  51.3 2.7 %collective-permute-start.6 = (f32[72,384]{1,0:T(8,128)S(1)}, f32[72,384]{1,0:T(8,128)S(1)}, u32[]{:S(2)}, u32[]{:S(2)}) collective-permute-start(f32[72,384]{1,0:T(8,128)S(1)} %add.75), channel_id=1, source_target_pairs={{0,16},{4,20},{8,24},{12,28},{16,0},{20,4},{24,8},{28,12},{1,17},{... | collective-permute-start | bytes 331784 | tf_op jit(solution)/shard_map/ppermute | solution.py:510
  53.9 4.2 %collective-permute-done.6 = f32[72,384]{1,0:T(8,128)S(1)} collective-permute-done((f32[72,384]{1,0:T(8,128)S(1)}, f32[72,384]{1,0:T(8,128)S(1)}, u32[]{:S(2)}, u32[]{:S(2)}) %collective-permute-start.6) | collective-permute-done | bytes 110624 | tf_op jit(solution)/shard_map/ppermute | solution.py:510
  58.2 0.1 collective-permute-start.7
  58.3 2.6 %blocks.4.refs_7_ = bf16[8,256,768]{2,1,0:T(8,128)(2,1)} custom-call(f32[8,6,544,128]{3,2,1,0:T(8,128)} %bitcast.1, f32[8,6,544,128]{3,2,1,0:T(8,128)} %bitcast.2, f32[8,6,544,128]{3,2,1,0:T(8,128)} %bitcast.3, f32[8,6,544,128]{3,2,1,0:T(8,128)} %bitcast.4, f32[8,6,544,128]{3,2,1,0:T(8,128)} %bitcast.5, f32[8,6,544,128]{3,2,1,0:T(8,128)} %bitcast.6, ...), custom_call_target="tpu_custom_call" | custom-call | flops 1769472 | bytes 2064384 | tf_op jit(solution)/shard_map/blocks/pallas_call | solution.py:431
  60.9 3.1 %blocks.5.refs_7_ = bf16[8,256,768]{2,1,0:T(8,128)(2,1)} custom-call(f32[8,6,544,128]{3,2,1,0:T(8,128)} %bitcast.12, f32[8,6,544,128]{3,2,1,0:T(8,128)} %bitcast.8, f32[8,6,544,128]{3,2,1,0:T(8,128)} %bitcast.9, f32[8,6,544,128]{3,2,1,0:T(8,128)} %bitcast.10, f32[8,6,544,128]{3,2,1,0:T(8,128)} %bitcast.11, ...), custom_call_target="tpu_custom_call", output_to_operand_aliasing={{}: (7, {})} | custom-call | flops 3538944 | bytes 4128768 | tf_op jit(solution)/shard_map/blocks/pallas_call | solution.py:431
  64.0 3.1 %blocks.6.refs_7_ = bf16[8,256,768]{2,1,0:T(8,128)(2,1)} custom-call(f32[8,6,544,128]{3,2,1,0:T(8,128)} %bitcast.13, f32[8,6,544,128]{3,2,1,0:T(8,128)} %bitcast.14, f32[8,6,544,128]{3,2,1,0:T(8,128)} %bitcast.15, f32[8,6,544,128]{3,2,1,0:T(8,128)} %bitcast.16, f32[8,6,544,128]{3,2,1,0:T(8,128)} %bitcast.17, ...), custom_call_target="tpu_custom_call", output_to_operand_aliasing={{}: (7, {})} | custom-call | flops 3538944 | bytes 4128768 | tf_op jit(solution)/shard_map/blocks/pallas_call | solution.py:431
  67.1 4.7 %blocks.7 = bf16[8,256,768]{2,1,0:T(8,128)(2,1)} custom-call(f32[8,6,544,128]{3,2,1,0:T(8,128)} %bitcast.19, f32[8,6,544,128]{3,2,1,0:T(8,128)} %bitcast.20, f32[8,6,544,128]{3,2,1,0:T(8,128)} %bitcast.21, f32[8,6,544,128]{3,2,1,0:T(8,128)} %bitcast.22, f32[8,6,544,128]{3,2,1,0:T(8,128)} %bitcast.23, ...), custom_call_target="tpu_custom_call", output_to_operand_aliasing={{}: (7, {})} | custom-call | flops 5308416 | bytes 6193152 | tf_op jit(solution)/shard_map/blocks/pallas_call | solution.py:431
  71.8 0.0 collective-permute-done.7
  71.8 0.6 slice_reduce_fusion
  72.4 0.6 slice.26
  73.0 0.7 slice.25
  (7 shorter events, 0.2 us)
Async XLA Ops:
  1.3 6.2 %collective-permute-start = (s32[8,128]{1,0:T(8,128)S(1)}, s32[8,128]{1,0:T(8,128)S(1)}, u32[]{:S(2)}, u32[]{:S(2)}) collective-permute-start(s32[8,128]{1,0:T(8,128)S(1)} %multiply_add_fusion), channel_id=1, source_target_pairs={{0,1},{1,2},{2,3},{4,5},{5,6},{6,7},{8,9},{9,10},{10,11},{12,13},{... | collective-permute-start | bytes 12296 | tf_op jit(solution)/shard_map/ppermute | solution.py:536
  7.5 0.6 copy-start
  33.1 2.0 %collective-permute-start.1 = (f32[264,384]{1,0:T(8,128)}, f32[264,384]{1,0:T(8,128)S(1)}, u32[]{:S(2)}, u32[]{:S(2)}) collective-permute-start(f32[264,384]{1,0:T(8,128)} %get-tuple-element.11), channel_id=1, source_target_pairs={{0,4},{4,0},{8,12},{12,8},{16,20},{20,16},{24,28},{28,24},{1,5},{5... | collective-permute-start | bytes 1216520 | tf_op jit(solution)/shard_map/ppermute | solution.py:510
  36.2 6.7 %collective-permute-start.2 = (f32[72,384]{1,0:T(8,128)S(1)}, f32[72,384]{1,0:T(8,128)S(1)}, u32[]{:S(2)}, u32[]{:S(2)}) collective-permute-start(f32[72,384]{1,0:T(8,128)S(1)} %get-tuple-element.16), channel_id=1, source_target_pairs={{0,1},{1,2},{2,3},{3,0},{4,5},{5,6},{6,7},{7,4},{8,9},{9,10},{10,1... | collective-permute-start | bytes 331784 | tf_op jit(solution)/shard_map/ppermute | solution.py:519
  38.5 6.7 %collective-permute-start.3 = (f32[72,384]{1,0:T(8,128)S(1)}, f32[72,384]{1,0:T(8,128)S(1)}, u32[]{:S(2)}, u32[]{:S(2)}) collective-permute-start(f32[72,384]{1,0:T(8,128)S(1)} %get-tuple-element.17), channel_id=1, source_target_pairs={{0,2},{1,3},{2,0},{3,1},{4,6},{5,7},{6,4},{7,5},{8,10},{9,11},{10,... | collective-permute-start | bytes 331784 | tf_op jit(solution)/shard_map/ppermute | solution.py:519
  40.1 6.4 %collective-permute-start.4 = (f32[72,384]{1,0:T(8,128)S(1)}, f32[72,384]{1,0:T(8,128)S(1)}, u32[]{:S(2)}, u32[]{:S(2)}) collective-permute-start(f32[72,384]{1,0:T(8,128)S(1)} %get-tuple-element.18), channel_id=1, source_target_pairs={{0,3},{1,0},{2,1},{3,2},{4,7},{5,4},{6,5},{7,6},{8,11},{9,8},{10,9... | collective-permute-start | bytes 331784 | tf_op jit(solution)/shard_map/ppermute | solution.py:519
  46.5 4.8 %collective-permute-start.5 = (f32[72,384]{1,0:T(8,128)S(1)}, f32[72,384]{1,0:T(8,128)S(1)}, u32[]{:S(2)}, u32[]{:S(2)}) collective-permute-start(f32[72,384]{1,0:T(8,128)S(1)} %fusion.2), channel_id=1, source_target_pairs={{0,8},{4,12},{8,0},{12,4},{16,24},{20,28},{24,16},{28,20},{1,9},{5... | collective-permute-start | bytes 331784 | tf_op jit(solution)/shard_map/ppermute | solution.py:510
  51.3 6.9 %collective-permute-start.6 = (f32[72,384]{1,0:T(8,128)S(1)}, f32[72,384]{1,0:T(8,128)S(1)}, u32[]{:S(2)}, u32[]{:S(2)}) collective-permute-start(f32[72,384]{1,0:T(8,128)S(1)} %add.75), channel_id=1, source_target_pairs={{0,16},{4,20},{8,24},{12,28},{16,0},{20,4},{24,8},{28,12},{1,17},{... | collective-permute-start | bytes 331784 | tf_op jit(solution)/shard_map/ppermute | solution.py:510
  58.2 13.6 %collective-permute-start.7 = (f32[72,384]{1,0:T(8,128)S(1)}, f32[72,384]{1,0:T(8,128)S(1)}, u32[]{:S(2)}, u32[]{:S(2)}) collective-permute-start(f32[72,384]{1,0:T(8,128)S(1)} %add.76), channel_id=1, source_target_pairs={{0,4},{4,0},{8,12},{12,8},{16,20},{20,16},{24,28},{28,24},{1,5},{5... | collective-permute-start | bytes 331784 | tf_op jit(solution)/shard_map/ppermute | solution.py:510
